TPU v7x, 128 devices: a whole 4x4x4 slice. The times are simulated.
128 devices in a mesh: ha: 16 (over x, z_hi, core), wa: 8 (over y, z_lo).
Axes of the slice: x: 4, y: 4, z: 4 (z_hi: 2, z_lo: 2; z = z_hi * 2 + z_lo), core: 2. Of those that a mesh axis runs over, the one named last changes fastest.
Arguments:
- frames: bfloat16 [2, 256, 512, 384], P(None, 'ha', 'wa'), may hold values from -6 to 6
- keep: int32 [2, 3], replicated, may hold values 0 or 1
- expand_weight: bfloat16 [384, 1536], replicated, may hold values from -0.3125 to 0.3125
- dw_kernel: float32 [3, 3, 1536], replicated, may hold values from -2 to 2
- conv_bias: float32 [1536], replicated, may hold values from -3 to 3
- project_weight: bfloat16 [1536, 384], replicated, may hold values from -0.15625 to 0.15625
- qkv_weight: bfloat16 [384, 1152], replicated, may hold values from -4 to 4
- out_weight: bfloat16 [384, 384], replicated, may hold values from -0.3125 to 0.3125
- mlp_in: bfloat16 [384, 1536], replicated, may hold values from -0.3125 to 0.3125
- mlp_out: bfloat16 [1536, 384], replicated, may hold values from -0.15625 to 0.15625
Outputs:
- result: bfloat16 [2, 256, 512, 384], P(None, 'ha', 'wa')
All inputs are finite; a program needn't handle non-finite values.
Results may differ from a plain program's by a relative error of at most 0.0068.
Values may be sent and summed in bfloat16 or wider, within the bound.
A program may use at most 64 MiB of HBM per device.

v0:
```python
import jax
import jax.numpy as jnp
from jax import lax
from jax.sharding import PartitionSpec as P

HEADS = 12
GRID = 16


def with_halo(x, sides, width):
    for axis, dim in sides:
        size, length = (lax.axis_size(axis), x.shape[dim])
        up = [(i, (i + 1) % size) for i in range(size - 1)]
        down = [(j, i) for i, j in up]
        last = lax.slice_in_dim(x, length - width, length, axis=dim)
        initial = lax.slice_in_dim(x, 0, width, axis=dim)
        before = lax.ppermute(last, axis, up)
        after = lax.ppermute(initial, axis, down)
        x = jnp.concatenate([before, x, after], axis=dim)
    return x


def normalize(values):
    mean_val = jnp.mean(values, axis=-1, keepdims=True)
    centred = values - mean_val
    variance = jnp.mean(centred * centred, axis=-1, keepdims=True)
    return centred * lax.rsqrt(variance + 1e-05)


def attend(block, window_flag, qkv_weight, out_weight):
    pair_count, token_count, channels = block.shape
    head_dim = channels // HEADS
    residual = block.astype(jnp.float32)
    normed = normalize(residual).astype(jnp.bfloat16)
    qkv = jnp.dot(normed, qkv_weight, preferred_element_type=jnp.float32).astype(jnp.bfloat16)
    queries = qkv[..., :channels].reshape(pair_count, token_count, HEADS, head_dim)
    keys_part = qkv[..., channels : 2 * channels].reshape(pair_count, token_count, HEADS, head_dim)
    values_part = qkv[..., 2 * channels :].reshape(pair_count, token_count, HEADS, head_dim)
    scores = jnp.einsum(
        "bqhd,bkhd->bhqk", queries, keys_part, preferred_element_type=jnp.float32
    ) * head_dim ** (-0.5)
    top_score = jnp.max(scores, axis=-1, keepdims=True)
    weights = jnp.exp(scores - top_score)
    probs = (weights / jnp.sum(weights, axis=-1, keepdims=True)).astype(jnp.bfloat16)
    attended = jnp.einsum("bhqk,bkhd->bqhd", probs, values_part, preferred_element_type=jnp.float32)
    attended = attended.astype(jnp.bfloat16).reshape(pair_count, token_count, channels)
    update = jnp.dot(attended, out_weight, preferred_element_type=jnp.float32)
    return (residual + window_flag[:, None, None] * update).astype(jnp.bfloat16)


def body(
    frames,
    keep,
    expand_weight,
    dw_kernel,
    conv_bias,
    project_weight,
    qkv_weight,
    out_weight,
    mlp_in,
    mlp_out,
):
    frame_count, row_count, col_count, channels = frames.shape
    rows_axis = lax.axis_size("ha")
    cols_axis = lax.axis_size("wa")
    flags = keep.astype(jnp.float32)
    expanded = jax.nn.gelu(
        jnp.dot(frames, expand_weight, preferred_element_type=jnp.float32)
    ).astype(jnp.bfloat16)
    padded = with_halo(expanded, (("ha", 1), ("wa", 2)), 1)
    total = jnp.zeros((frame_count, row_count, col_count, padded.shape[-1]), jnp.float32)
    for shift_y in range(3):
        for shift_x in range(3):
            total = (
                total
                + padded[:, shift_y : shift_y + row_count, shift_x : shift_x + col_count, :].astype(
                    jnp.float32
                )
                * dw_kernel[shift_y, shift_x]
            )
    mixed = jax.nn.gelu(total + conv_bias).astype(jnp.bfloat16)
    branch = jnp.dot(mixed, project_weight, preferred_element_type=jnp.float32)
    first = (frames.astype(jnp.float32) + flags[:, 0][:, None, None, None] * branch).astype(
        jnp.bfloat16
    )
    row_stride = row_count * rows_axis // GRID
    col_stride = col_count * cols_axis // GRID
    rows_each = row_stride // rows_axis
    cols_each = col_stride // cols_axis
    row_groups = row_count // row_stride
    col_groups = col_count // col_stride
    outgoing = first.reshape(
        frame_count, row_groups, rows_axis, rows_each, col_groups, cols_axis, cols_each, channels
    )
    outgoing = outgoing.transpose(0, 2, 5, 3, 6, 1, 4, 7)
    flat_send = outgoing.reshape(
        frame_count, rows_axis * cols_axis, rows_each, cols_each, row_groups, col_groups, channels
    )
    arrived = lax.all_to_all(flat_send, ("ha", "wa"), split_axis=1, concat_axis=1, tiled=True)
    arrived = arrived.reshape(
        frame_count, rows_axis, cols_axis, rows_each, cols_each, row_groups, col_groups, channels
    )
    windows = arrived.transpose(0, 3, 4, 1, 5, 2, 6, 7).reshape(-1, GRID * GRID, channels)
    window_count = windows.shape[0]
    window_flags = jnp.repeat(flags[:, 1], window_count // frame_count).reshape(
        window_count // 2, 2
    )
    blocks = windows.reshape(window_count // 2, 2, GRID * GRID, channels)

    def one_pair(pair):
        return attend(pair[0], pair[1], qkv_weight, out_weight)

    second = lax.map(one_pair, (blocks, window_flags))
    second = second.reshape(
        frame_count, rows_each, cols_each, rows_axis, row_groups, cols_axis, col_groups, channels
    )
    second = second.transpose(0, 3, 5, 1, 2, 4, 6, 7)
    flat_back = second.reshape(
        frame_count, rows_axis * cols_axis, rows_each, cols_each, row_groups, col_groups, channels
    )
    returned = lax.all_to_all(flat_back, ("ha", "wa"), split_axis=1, concat_axis=1, tiled=True)
    returned = returned.reshape(
        frame_count, rows_axis, cols_axis, rows_each, cols_each, row_groups, col_groups, channels
    )
    restored = returned.transpose(0, 5, 1, 3, 6, 2, 4, 7).reshape(
        frame_count, row_count, col_count, channels
    )
    residual = restored.astype(jnp.float32)
    normed = normalize(residual).astype(jnp.bfloat16)
    inner = jax.nn.gelu(jnp.dot(normed, mlp_in, preferred_element_type=jnp.float32)).astype(
        jnp.bfloat16
    )
    update = jnp.dot(inner, mlp_out, preferred_element_type=jnp.float32)
    return (residual + flags[:, 2][:, None, None, None] * update).astype(jnp.bfloat16)


def solution(mesh):
    in_specs = (P(None, "ha", "wa", None), P(), P(), P(), P(), P(), P(), P(), P(), P())
    out_specs = P(None, "ha", "wa", None)
    return jax.shard_map(body, mesh=mesh, in_specs=in_specs, out_specs=out_specs, check_vma=False)
```

profile of v0, /device:TPU:1, one launch (start us, length us, event | category | flops | bytes accessed | tf_op | source)
XLA Modules:
  0.0 216.3 jit_solution(14953704426492121213)
XLA Ops:
  0.0 1.3 copy-done
  1.3 6.8 %fusion.34 = bf16[2,16,64,1536]{3,2,1,0:T(8,128)(2,1)S(1)} fusion(bf16[2,16,64,384]{3,2,1,0:T(8,128)(2,1)} %param.12, bf16[384,1536]{1,0:T(8,128)(2,1)S(1)} %copy-done), kind=kOutput, calls=%fused_computation.43 | convolution fusion | flops 2444230656 | bytes 9043968 | tf_op jit(solution)/shard_map/dot_general | solution.py:68
  8.1 6.9 %collective-permute-start = (bf16[2,1,64,1536]{3,2,1,0:T(8,128)(2,1)S(1)}, bf16[2,1,64,1536]{3,2,1,0:T(8,128)(2,1)S(1)}, u32[]{:S(2)}, u32[]{:S(2)}) collective-permute-start(bf16[2,1,64,1536]{3,2,1,0:T(8,128)(2,1)S(1)} %get-tuple-element.71), channel_id=1, source_target_pairs={{0,8},{8,16},{16,24},{24,32},{32,40},{40,48},{48,56},{56,64},{64,7... | collective-permute-start | bytes 1179656 | tf_op jit(solution)/shard_map/ppermute | solution.py:17
  15.0 1.9 collective-permute-start.1
  17.1 7.2 %collective-permute-done = bf16[2,1,64,1536]{3,2,1,0:T(8,128)(2,1)S(1)} collective-permute-done((bf16[2,1,64,1536]{3,2,1,0:T(8,128)(2,1)S(1)}, bf16[2,1,64,1536]{3,2,1,0:T(8,128)(2,1)S(1)}, u32[]{:S(2)}, u32[]{:S(2)}) %collective-permute-start) | collective-permute-done | bytes 393248 | tf_op jit(solution)/shard_map/ppermute | solution.py:17
  24.3 1.3 collective-permute-done.1
  25.6 0.3 pad_maximum_fusion.5
  26.0 2.7 %collective-permute-start.2 = (bf16[2,18,1,1536]{3,2,1,0:T(2,128)(2,1)S(1)}, bf16[2,18,1,1536]{3,2,1,0:T(2,128)(2,1)S(1)}, u32[]{:S(2)}, u32[]{:S(2)}) collective-permute-start(bf16[2,18,1,1536]{3,2,1,0:T(2,128)(2,1)S(1)} %get-tuple-element.69), channel_id=1, source_target_pairs={{0,1},{1,2},{2,3},{3,4},{4,5},{5,6},{6,7},{8,9},{9,10},{10,11},{11... | collective-permute-start | bytes 331784 | tf_op jit(solution)/shard_map/ppermute | solution.py:17
  28.6 1.3 collective-permute-start.3
  30.2 2.0 collective-permute-done.2
  32.2 3.4 %collective-permute-done.3 = bf16[2,18,1,1536]{3,2,1,0:T(2,128)(2,1)S(1)} collective-permute-done((bf16[2,18,1,1536]{3,2,1,0:T(2,128)(2,1)S(1)}, bf16[2,18,1,1536]{3,2,1,0:T(2,128)(2,1)S(1)}, u32[]{:S(2)}, u32[]{:S(2)}) %collective-permute-start.3) | collective-permute-done | bytes 110624 | tf_op jit(solution)/shard_map/ppermute | solution.py:18
  35.6 6.3 %maximum_maximum_fusion = (bf16[2,18,65,1536]{3,2,1,0:T(8,128)(2,1)S(1)}, bf16[2,18,65,1536]{3,2,1,0:T(8,128)(2,1)}) fusion(bf16[2,1,64,1536]{3,2,1,0:T(8,128)(2,1)S(1)} %collective-permute-done.1, bf16[2,16,64,1536]{3,2,1,0:T(8,128)(2,1)S(1)} %fusion.34, bf16[2,1,64,1536]{3,2,1,0:T(8,128)(2,1)S(1)} %collective-permute-done, ...), kind=kLoop, calls=%fused_computation.60 | loop fusion | flops 57507840 | bytes 21676032 | tf_op jit(solution)/shard_map/concatenate | solution.py:19
  41.9 24.8 %add_convert_fusion.1 = bf16[2,16,64,384]{3,2,1,0:T(8,128)(2,1)S(1)} fusion(bf16[2,16,64,384]{3,2,1,0:T(8,128)(2,1)S(1)} %copy-done.4, bf16[2,16,64,1536]{3,2,1,0:T(8,128)(2,1)S(1)} %fusion.34, bf16[2,18,65,1536]{3,2,1,0:T(8,128)(2,1)} %get-tuple-element.68, bf16[2,1,64,1536]{3,2,1,0:T(8,128)(2,1)S(1)} %collective-permute-done.1, ...), kind=kOutput, calls=%fused_computation.69 | convolution fusion | flops 2538602496 | bytes 49234432 | tf_op jit(solution)/shard_map/dot_general | solution.py:82
  66.7 0.4 reshape.94
  67.4 2.8 %copy.49 = bf16[2,128,1,4,1,2,384]{6,5,3,0,4,2,1:T(2,128)(2,1)} copy(bf16[2,128,1,4,1,2,384]{6,1,5,3,0,4,2:T(8,128)(2,1)S(1)} %bitcast.127) | data formatting | bytes 3145728 | tf_op jit(solution)/shard_map/reshape | solution.py:96
  70.2 13.0 %all-to-all-start = ((bf16[2,128,1,4,1,2,384]{6,5,3,0,4,2,1:T(2,128)(2,1)}), bf16[2,128,1,4,1,2,384]{6,5,3,0,4,2,1:T(2,128)(2,1)S(1)}, u32[]{:S(2)}, u32[]{:S(2)}) async-start(bf16[2,128,1,4,1,2,384]{6,5,3,0,4,2,1:T(2,128)(2,1)} %copy.49), calls=%async_computation | async-start | bytes 3145728 | tf_op jit(solution)/shard_map/all_to_all | solution.py:99
  83.3 24.4 %all-to-all-done = bf16[2,128,1,4,1,2,384]{6,5,3,0,4,2,1:T(2,128)(2,1)S(1)} async-done(((bf16[2,128,1,4,1,2,384]{6,5,3,0,4,2,1:T(2,128)(2,1)}), bf16[2,128,1,4,1,2,384]{6,5,3,0,4,2,1:T(2,128)(2,1)S(1)}, u32[]{:S(2)}, u32[]{:S(2)}) %all-to-all-start) | async-done | bytes 1572896 | tf_op jit(solution)/shard_map/all_to_all | solution.py:99
  107.7 2.4 %copy.50 = bf16[2,1,4,16,1,8,2,384]{7,6,5,3,2,0,4,1:T(2,128)(2,1)} copy(bf16[2,1,4,16,1,8,2,384]{7,6,2,0,5,3,4,1:T(2,128)(2,1)S(1)} %bitcast.126) | data formatting | bytes 3145728 | tf_op jit(solution)/shard_map/transpose | solution.py:103
  110.1 3.7 %reshape_reshape.4 = bf16[4,2,256,384]{3,2,1,0:T(8,128)(2,1)S(1)} reshape(bf16[2,1,4,16,1,8,2,384]{7,6,5,3,2,0,4,1:T(2,128)(2,1)} %copy.50) | data formatting | bytes 3145728 | tf_op jit(solution)/shard_map/reshape;reshape | solution.py:108
  113.8 50.9 %while.10 = (s32[]{:T(128)}, bf16[4,2,256,384]{3,2,1,0:T(8,128)(2,1)}, bf16[4,2,256,384]{3,2,1,0:T(8,128)(2,1)S(1)}, f32[4,2]{1,0:T(4,128)S(1)}, bf16[384,1152]{...) while((s32[]{:T(128)}, bf16[4,2,256,384]{3,2,1,0:T(8,128)(2,1)}, ...), condition=%wide.region_5.6_spmd, body=%wide.region_0.5_spmd.sunk | while | flops 816710400 | bytes 23661172 | solution.py:113
  114.0 0.3 fusion.105
  114.3 2.0 convolution_convert_fusion.2
  116.8 4.9 %fusion.107 = (f32[2,12,256]{2,1,0:T(8,128)S(1)}, f32[2,12,256,256]{2,3,1,0:T(8,128)}) fusion(bf16[2,256,12,32]{1,3,2,0:T(8,128)(2,1)S(1)} %bitcast.123, bf16[2,256,12,32]{1,3,2,0:T(8,128)(2,1)S(1)} %bitcast.124), kind=kOutput, calls=%fused_computation.106.clone.1 | convolution fusion | flops 105382144 | bytes 7102464 | tf_op jit(solution)/shard_map/while/body/eval_jaxpr/sub | solution.py:43
  121.9 3.4 %fusion.108 = bf16[2,12,32,256]{3,2,1,0:T(8,128)(2,1)S(1)} fusion(bf16[2,256,12,32]{1,3,2,0:T(8,128)(2,1)S(1)} %bitcast.125, f32[2,12,256,256]{2,3,1,0:T(8,128)} %get-tuple-element.118, f32[2,12,256]{2,1,0:T(8,128)S(1)} %get-tuple-element.119), kind=kOutput, calls=%fused_computation.11.clone.1 | convolution fusion | flops 104005632 | bytes 7102464 | tf_op jit(solution)/shard_map/while/body/eval_jaxpr/bhqk,bkhd->bqhd/dot_general | solution.py:45
  125.3 1.2 fusion.110
  126.7 0.3 fusion.105
  127.0 2.0 convolution_convert_fusion.2
  129.6 4.9 %fusion.107 = (f32[2,12,256]{2,1,0:T(8,128)S(1)}, f32[2,12,256,256]{2,3,1,0:T(8,128)}) fusion(bf16[2,256,12,32]{1,3,2,0:T(8,128)(2,1)S(1)} %bitcast.123, bf16[2,256,12,32]{1,3,2,0:T(8,128)(2,1)S(1)} %bitcast.124), kind=kOutput, calls=%fused_computation.106.clone.1 | convolution fusion | flops 105382144 | bytes 7102464 | tf_op jit(solution)/shard_map/while/body/eval_jaxpr/sub | solution.py:43
  134.6 3.4 %fusion.108 = bf16[2,12,32,256]{3,2,1,0:T(8,128)(2,1)S(1)} fusion(bf16[2,256,12,32]{1,3,2,0:T(8,128)(2,1)S(1)} %bitcast.125, f32[2,12,256,256]{2,3,1,0:T(8,128)} %get-tuple-element.118, f32[2,12,256]{2,1,0:T(8,128)S(1)} %get-tuple-element.119), kind=kOutput, calls=%fused_computation.11.clone.1 | convolution fusion | flops 104005632 | bytes 7102464 | tf_op jit(solution)/shard_map/while/body/eval_jaxpr/bhqk,bkhd->bqhd/dot_general | solution.py:45
  138.1 1.2 fusion.110
  139.5 0.3 fusion.105
  139.7 2.0 convolution_convert_fusion.2
  142.3 4.9 %fusion.107 = (f32[2,12,256]{2,1,0:T(8,128)S(1)}, f32[2,12,256,256]{2,3,1,0:T(8,128)}) fusion(bf16[2,256,12,32]{1,3,2,0:T(8,128)(2,1)S(1)} %bitcast.123, bf16[2,256,12,32]{1,3,2,0:T(8,128)(2,1)S(1)} %bitcast.124), kind=kOutput, calls=%fused_computation.106.clone.1 | convolution fusion | flops 105382144 | bytes 7102464 | tf_op jit(solution)/shard_map/while/body/eval_jaxpr/sub | solution.py:43
  147.3 3.4 %fusion.108 = bf16[2,12,32,256]{3,2,1,0:T(8,128)(2,1)S(1)} fusion(bf16[2,256,12,32]{1,3,2,0:T(8,128)(2,1)S(1)} %bitcast.125, f32[2,12,256,256]{2,3,1,0:T(8,128)} %get-tuple-element.118, f32[2,12,256]{2,1,0:T(8,128)S(1)} %get-tuple-element.119), kind=kOutput, calls=%fused_computation.11.clone.1 | convolution fusion | flops 104005632 | bytes 7102464 | tf_op jit(solution)/shard_map/while/body/eval_jaxpr/bhqk,bkhd->bqhd/dot_general | solution.py:45
  150.8 1.2 fusion.110
  152.5 2.0 convolution_convert_fusion.2
  155.0 4.9 %fusion.107 = (f32[2,12,256]{2,1,0:T(8,128)S(1)}, f32[2,12,256,256]{2,3,1,0:T(8,128)}) fusion(bf16[2,256,12,32]{1,3,2,0:T(8,128)(2,1)S(1)} %bitcast.123, bf16[2,256,12,32]{1,3,2,0:T(8,128)(2,1)S(1)} %bitcast.124), kind=kOutput, calls=%fused_computation.106.clone.1 | convolution fusion | flops 105382144 | bytes 7102464 | tf_op jit(solution)/shard_map/while/body/eval_jaxpr/sub | solution.py:43
  160.1 3.4 %fusion.108 = bf16[2,12,32,256]{3,2,1,0:T(8,128)(2,1)S(1)} fusion(bf16[2,256,12,32]{1,3,2,0:T(8,128)(2,1)S(1)} %bitcast.125, f32[2,12,256,256]{2,3,1,0:T(8,128)} %get-tuple-element.118, f32[2,12,256]{2,1,0:T(8,128)S(1)} %get-tuple-element.119), kind=kOutput, calls=%fused_computation.11.clone.1 | convolution fusion | flops 104005632 | bytes 7102464 | tf_op jit(solution)/shard_map/while/body/eval_jaxpr/bhqk,bkhd->bqhd/dot_general | solution.py:45
  163.5 1.2 fusion.110
  164.7 3.5 %reshape.97 = bf16[2,1,4,16,1,8,2,384]{7,6,5,3,2,0,4,1:T(2,128)(2,1)S(1)} reshape(bf16[4,2,256,384]{3,2,1,0:T(8,128)(2,1)} %get-tuple-element.37) | data formatting | bytes 3145728 | tf_op jit(solution)/shard_map/reshape | solution.py:114
  168.3 1.4 copy.51
  169.7 29.2 %all_to_all.10 = bf16[2,128,1,4,1,2,384]{6,5,3,0,4,2,1:T(2,128)(2,1)S(1)} all-to-all(bf16[2,128,1,4,1,2,384]{6,5,3,0,4,2,1:T(2,128)(2,1)S(1)} %bitcast.128), channel_id=1, replica_groups=mesh['ha'=16,'wa'=8] {'ha','wa'}, dimensions={1} | all-to-all | bytes 3145728 | tf_op jit(solution)/shard_map/all_to_all | solution.py:121
  198.9 0.4 fusion.56
  199.5 0.9 multiply_reduce_fusion.1
  200.6 0.4 convert_bitcast_fusion.1
  201.0 2.0 copy.53
  203.0 2.3 %reshape.99 = f32[2,16,64,384]{3,2,1,0:T(8,128)} reshape(f32[2,1,16,1,2,8,4,384]{7,6,5,4,2,0,3,1:T(4,128)S(1)} %copy.53) | data formatting | bytes 6291456 | tf_op jit(solution)/shard_map/convert_element_type | solution.py:128
  205.3 10.9 %add_convert_fusion = bf16[2,16,64,384]{3,2,1,0:T(8,128)(2,1)} fusion(f32[2,16,64,384]{3,2,1,0:T(8,128)} %reshape.99, f32[2,16,64]{2,1,0:T(8,128)S(1)} %copy.60, f32[2,16,64]{2,1,0:T(8,128)S(1)} %copy.56, f32[2]{0:T(128)S(1)} %get-tuple-element.47, bf16[1536,384]{1,0:T(8,128)(2,1)} %param.21, bf16[384,1536]{1,0:T(8,128)(2,1)} %param.20), kind=kOutput, calls=%fused_computation.66 | convolution fusion | flops 4864868352 | bytes 7094280 | tf_op jit(solution)/shard_map/dot_general | solution.py:133
  (66 shorter events, 5.0 us)
Async XLA Ops:
  0.0 1.3 copy-start
  0.0 16.9 %copy-start.3 = (s32[2,3]{1,0:T(2,128)S(1)}, s32[2,3]{1,0:T(2,128)}, u32[]{:S(2)}) copy-start(s32[2,3]{1,0:T(2,128)} %param.13) | copy-start | bytes 76
  0.0 17.0 %copy-start.2 = (f32[3,3,1536]{2,1,0:T(4,128)S(1)}, f32[3,3,1536]{2,1,0:T(4,128)}, u32[]{:S(2)}) copy-start(f32[3,3,1536]{2,1,0:T(4,128)} %param.15) | copy-start | bytes 165892
  8.1 16.2 %collective-permute-start = (bf16[2,1,64,1536]{3,2,1,0:T(8,128)(2,1)S(1)}, bf16[2,1,64,1536]{3,2,1,0:T(8,128)(2,1)S(1)}, u32[]{:S(2)}, u32[]{:S(2)}) collective-permute-start(bf16[2,1,64,1536]{3,2,1,0:T(8,128)(2,1)S(1)} %get-tuple-element.71), channel_id=1, source_target_pairs={{0,8},{8,16},{16,24},{24,32},{32,40},{40,48},{48,56},{56,64},{64,7... | collective-permute-start | bytes 1179656 | tf_op jit(solution)/shard_map/ppermute | solution.py:17
  15.0 10.6 %collective-permute-start.1 = (bf16[2,1,64,1536]{3,2,1,0:T(8,128)(2,1)S(1)}, bf16[2,1,64,1536]{3,2,1,0:T(8,128)(2,1)S(1)}, u32[]{:S(2)}, u32[]{:S(2)}) collective-permute-start(bf16[2,1,64,1536]{3,2,1,0:T(8,128)(2,1)S(1)} %get-tuple-element.72), channel_id=1, source_target_pairs={{8,0},{16,8},{24,16},{32,24},{40,32},{48,40},{56,48},{64,56},{72,6... | collective-permute-start | bytes 1179656 | tf_op jit(solution)/shard_map/ppermute | solution.py:18
  26.0 6.2 %collective-permute-start.2 = (bf16[2,18,1,1536]{3,2,1,0:T(2,128)(2,1)S(1)}, bf16[2,18,1,1536]{3,2,1,0:T(2,128)(2,1)S(1)}, u32[]{:S(2)}, u32[]{:S(2)}) collective-permute-start(bf16[2,18,1,1536]{3,2,1,0:T(2,128)(2,1)S(1)} %get-tuple-element.69), channel_id=1, source_target_pairs={{0,1},{1,2},{2,3},{3,4},{4,5},{5,6},{6,7},{8,9},{9,10},{10,11},{11... | collective-permute-start | bytes 331784 | tf_op jit(solution)/shard_map/ppermute | solution.py:17
  28.6 7.0 %collective-permute-start.3 = (bf16[2,18,1,1536]{3,2,1,0:T(2,128)(2,1)S(1)}, bf16[2,18,1,1536]{3,2,1,0:T(2,128)(2,1)S(1)}, u32[]{:S(2)}, u32[]{:S(2)}) collective-permute-start(bf16[2,18,1,1536]{3,2,1,0:T(2,128)(2,1)S(1)} %get-tuple-element.70), channel_id=1, source_target_pairs={{1,0},{2,1},{3,2},{4,3},{5,4},{6,5},{7,6},{9,8},{10,9},{11,10},{12... | collective-permute-start | bytes 331784 | tf_op jit(solution)/shard_map/ppermute | solution.py:18
  30.1 11.8 %copy-start.4 = (bf16[2,16,64,384]{3,2,1,0:T(8,128)(2,1)S(1)}, bf16[2,16,64,384]{3,2,1,0:T(8,128)(2,1)}, u32[]{:S(2)}) copy-start(bf16[2,16,64,384]{3,2,1,0:T(8,128)(2,1)} %param.12) | copy-start | bytes 4718596
  30.2 11.7 %copy-start.5 = (bf16[1536,384]{1,0:T(8,128)(2,1)S(1)}, bf16[1536,384]{1,0:T(8,128)(2,1)}, u32[]{:S(2)}) copy-start(bf16[1536,384]{1,0:T(8,128)(2,1)} %param.17) | copy-start | bytes 3538948
  30.2 11.7 %copy-start.7 = (f32[1536]{0:T(1024)S(1)}, f32[1536]{0:T(1024)}, u32[]{:S(2)}) copy-start(f32[1536]{0:T(1024)} %param.16) | copy-start | bytes 18436
  67.4 46.5 %copy-start.6 = (bf16[384,384]{1,0:T(8,128)(2,1)S(1)}, bf16[384,384]{1,0:T(8,128)(2,1)}, u32[]{:S(2)}) copy-start(bf16[384,384]{1,0:T(8,128)(2,1)} %param.19) | copy-start | bytes 884740
  70.2 37.6 %all-to-all-start = ((bf16[2,128,1,4,1,2,384]{6,5,3,0,4,2,1:T(2,128)(2,1)}), bf16[2,128,1,4,1,2,384]{6,5,3,0,4,2,1:T(2,128)(2,1)S(1)}, u32[]{:S(2)}, u32[]{:S(2)}) async-start(bf16[2,128,1,4,1,2,384]{6,5,3,0,4,2,1:T(2,128)(2,1)} %copy.49), calls=%async_computation | async-start | bytes 3145728 | tf_op jit(solution)/shard_map/all_to_all | solution.py:99
  205.3 10.9 %copy-start.1 = (bf16[384,1536]{1,0:T(8,128)(2,1)S(1)}, bf16[384,1536]{1,0:T(8,128)(2,1)}, u32[]{:S(2)}) copy-start(bf16[384,1536]{1,0:T(8,128)(2,1)} %param.14) | copy-start | bytes 3538948
where the time goes:
time: 217 us; the launch traced here: 216 us
  matrix products  88.8 us (41%)
  waiting for transfers between devices  38.3 us (18%)
  blocking collectives  29.2 us (13%)
  starting transfers between devices  25.8 us (12%)
  local copies, waits for them, and re-layouts  23.7 us (11%)
  other arithmetic  10 us (5%)
    all_to_all x1, blocking collectives, body(): lax.all_to_all(flat_back, ('ha', 'wa'), split_axis=1, concat_axis=1, tile...  29.2 us
    dot_general x1, matrix products, body(): branch = jnp.dot(mixed, project_weight, preferred_element_type=jnp.float32)  24.8 us
    all_to_all x1, waiting for transfers between devices, body(): lax.all_to_all(flat_send, ('ha', 'wa'), split_axis=1, concat_axis=1, tile...  24.4 us
    sub x4, matrix products, attend(): weights = jnp.exp(scores - top_score)  19.5 us
    dot_general x4, matrix products, attend(): jnp.einsum('bhqk,bkhd->bqhd', probs, values_part, preferred_element_type=...  13.8 us
    all_to_all x1, starting transfers between devices, body(): lax.all_to_all(flat_send, ('ha', 'wa'), split_axis=1, concat_axis=1, tile...  13 us
    dot_general x1, matrix products, body(): update = jnp.dot(inner, mlp_out, preferred_element_type=jnp.float32)  10.9 us
    ppermute x2, starting transfers between devices, with_halo(): before = lax.ppermute(last, axis, up)  9.54 us
  transfers between devices with their start and end apart: 5, of which 5 were waited for; matrix products, arithmetic and copies ran while one was open for 0% of the time, Pallas kernels for 0%

commit v1 on v0

v1 whole, which is shorter than its diff:
```python
import functools
import math

import jax
import jax.numpy as jnp
from jax import lax
from jax.experimental import pallas as pl
from jax.experimental.pallas import tpu as pltpu
from jax.sharding import PartitionSpec as P

MESH = pl.DeviceIdType.MESH
F32, BF16 = jnp.float32, jnp.bfloat16
HA, WA = 16, 8
DEV = HA * WA
FR, RO, CO, C, EX = 2, 16, 64, 384, 1536
HEADS, HD = 12, 32
CH = 256
GA, GB = math.sqrt(2 / math.pi), math.sqrt(2 / math.pi) * 0.044715


def gelu(v):
    half = 0.5 * v
    return half + half * jnp.tanh(v * (GA + GB * (v * v)))


def norm(v):
    c = v - jnp.mean(v, axis=-1, keepdims=True)
    return (c * lax.rsqrt(jnp.mean(c * c, axis=-1, keepdims=True) + 1e-05)).astype(BF16)


def put(ref, rows, value):
    for l in range(3):
        ref[l, rows, :] = value[:, 128 * l : 128 * l + 128]


def take(ref, rows):
    return jnp.concatenate([ref[l, rows, :] for l in range(3)], 1)


def dot(a, b):
    return jnp.dot(a, b, preferred_element_type=F32)


def kernel(
    x, keep, we, dwk, bias, wp, wqkv, wo, wi, w2, out,
    xp, cols, hb, e, kb, le, mx, s, r, z, o, t, fs,
    halo_send, halo_recv, s_send, s_recv, z_send, z_recv, entry,
):
    ha, wa = lax.axis_index("ha"), lax.axis_index("wa")
    me = ha * WA + wa
    own_x, own_g = ha // 4, lax.rem(ha, 4)

    def at(h, w):
        return {"ha": h, "wa": w}

    barrier = pltpu.get_barrier_semaphore()
    near = [(lax.rem(ha + i, HA), wa) for i in range(1, HA)]
    near += [(ha, lax.rem(wa + i, WA)) for i in range(1, WA)]
    for h, w in near:
        pl.semaphore_signal(barrier, 1, device_id=at(h, w), device_id_type=MESH)

    for k in range(9):
        kb[k] = jnp.broadcast_to(dwk[k : k + 1, :], (8, EX))
    kb[9] = jnp.broadcast_to(bias[...], (8, EX))

    def permute(f, _):
        put(t, slice(None), x[f].astype(F32).reshape(RO * CO, C))

        def one(row, _):
            for q in range(0, 8, 2):
                two = [take(t, pl.ds(row * CO + q + i, 8, stride=8)) for i in range(2)]
                xp[f, row, q * 8 : q * 8 + 16, :] = jnp.concatenate(two, 0).astype(BF16)
            return 0

        lax.fori_loop(0, RO, one, 0)
        for side in range(2):
            cols[side, f] = take(t, pl.ds(side * (CO - 1), RO, stride=CO)).astype(BF16)
        return 0

    lax.fori_loop(0, FR, permute, 0)

    pl.semaphore_wait(barrier, len(near))
    for h, w in near[HA - 1 :]:
        pl.semaphore_signal(entry, 1, device_id=at(h, w), device_id_type=MESH)

    def expand(f, _):
        def rows(q, _):
            tokens = xp[f, pl.ds(q * 4, 4)].reshape(256, C)
            for n in range(0, EX, CH):
                v = gelu(dot(tokens, we[:, n : n + CH]))
                e[f, pl.ds(q * 4 + 1, 4), 1:9, :, n : n + CH] = v.reshape(4, 8, 8, CH)
            return 0

        return lax.fori_loop(0, 4, rows, 0)

    expand(0, 0)
    pl.semaphore_wait(entry, WA - 1)

    up, down = lax.rem(ha + HA - 1, HA), lax.rem(ha + 1, HA)
    left, right = lax.rem(wa + WA - 1, WA), lax.rem(wa + 1, WA)

    def halo(f):
        moves = [
            (xp.at[f, RO - 1], hb.at[f, 0:64], (down, wa)),
            (xp.at[f, 0], hb.at[f, 64:128], (up, wa)),
        ]
        for side, w in ((1, right), (0, left)):
            for blk, h in ((0, down), (1, ha), (2, up)):
                first = 128 + (1 - side) * 48 + blk * 16
                moves.append((cols.at[side, f], hb.at[f, first : first + 16], (h, w)))
        return [
            pltpu.make_async_remote_copy(
                src, dst, halo_send.at[f, i], halo_recv.at[f, i], device_id=at(*to), device_id_type=MESH
            )
            for i, (src, dst, to) in enumerate(moves)
        ]

    halos = [halo(f) for f in range(FR)]
    for f in range(FR):
        for c in halos[f]:
            c.start()
    expand(1, 0)
    for f in range(FR):
        for c in halos[f]:
            c.wait()

    ok_up, ok_down = (ha > 0).astype(F32), (ha < HA - 1).astype(F32)
    ok_side = ((wa > 0).astype(F32), (wa < WA - 1).astype(F32))
    sub = lax.broadcasted_iota(jnp.int32, (8, EX), 0)

    def edges(f, _):
        tokens = hb[f]
        for n in range(0, EX, CH):
            v = gelu(dot(tokens, we[:, n : n + CH]))
            e[f, 0, 1:9, :, n : n + CH] = (v[0:64] * ok_up).reshape(8, 8, CH)
            e[f, RO + 1, 1:9, :, n : n + CH] = (v[64:128] * ok_down).reshape(8, 8, CH)
            for side in range(2):
                p = 128 + side * 48
                le[side, 0:16, n : n + CH] = v[p : p + 16] * (ok_side[side] * ok_up)
                le[side, 16:32, n : n + CH] = v[p + 16 : p + 32] * ok_side[side]
                le[side, 32:48, n : n + CH] = v[p + 32 : p + 48] * (ok_side[side] * ok_down)

        def fill(p, _):
            a = pltpu.roll(e[f, p, 8], 1, 0)
            e[f, p, 0] = jnp.where(sub == 0, jnp.broadcast_to(le[0, pl.ds(15 + p, 1), :], (8, EX)), a)
            b = pltpu.roll(e[f, p, 1], 7, 0)
            e[f, p, 9] = jnp.where(sub == 7, jnp.broadcast_to(le[1, pl.ds(15 + p, 1), :], (8, EX)), b)
            return 0

        lax.fori_loop(0, RO + 2, fill, 0)
        return 0

    lax.fori_loop(0, FR, edges, 0)

    def partner(i, g, k):
        h, w = lax.rem(own_x + i, 4) * 4 + g, lax.rem(wa + k, WA)
        return h, w

    def spread(src, dst, send, recv, f, g, gg):
        for i in range(4):
            for k in range(8):
                h, w = partner(i, g, k)
                copy = pltpu.make_async_remote_copy(
                    src.at[f, h * WA + w], dst.at[f, me], send.at[f], recv.at[f],
                    device_id=at(h, w), device_id_type=MESH,
                )
                if i == 0 and k == 0:

                    @pl.when(gg > 0)
                    def _():
                        copy.start()
                else:
                    copy.start()

    def arrived(src, dst, send, recv, f):
        return pltpu.make_async_remote_copy(
            src.at[f, 0 : DEV - 1], dst.at[f, 0 : DEV - 1], send.at[f], recv.at[f],
            device_id=at(ha, wa), device_id_type=MESH,
        )

    def conv(f, _):
        flag = keep[f, 0].astype(F32)

        def group(gg, _):
            g = lax.rem(own_g + gg, 4)

            def row(rr, _):
                y = g * 4 + rr
                for n in range(0, EX, 128):
                    acc = jnp.broadcast_to(kb[9, :, n : n + 128][None], (8, 8, 128))
                    for i in range(3):
                        for j in range(3):
                            acc = acc + e[f, y + i, j : j + 8, :, n : n + 128] * kb[3 * i + j, :, n : n + 128][None]
                    mx[pl.ds(rr * 64, 64), n : n + 128] = gelu(acc).reshape(64, 128).astype(BF16)
                return 0

            lax.fori_loop(0, 4, row, 0)
            tokens = xp[f, pl.ds(g * 4, 4)].reshape(256, C)
            put(fs, slice(None), tokens.astype(F32) + flag * dot(mx[...], wp[...]))
            for i in range(4):
                for k in range(8):
                    part = take(fs, pl.ds(i * 64 + (k % 2) * 32 + k // 2, 8, stride=4))
                    s[f, (i * 4 + g) * WA + k] = part.astype(BF16)
            spread(s, r, s_send, s_recv, f, g, gg)
            return 0

        lax.fori_loop(0, 4, group, 0)
        r[f, me] = s[f, me]
        return 0

    lax.fori_loop(0, FR, conv, 0)

    lane = lax.broadcasted_iota(jnp.int32, (256, 128), 1)
    ones = jnp.ones((256, 128), BF16)
    expo = HD**-0.5 * math.log2(math.e)

    def attention(f, _):
        arrived(s, r, s_send, s_recv, f).wait_recv()
        put(t, slice(None), r[f].astype(F32).reshape(DEV * 8, C))
        flag, flag_two = keep[f, 1].astype(F32), keep[f, 2].astype(F32)

        def window(j, _):
            first = jnp.concatenate([take(t, pl.ds(2 * j + h, DEV, stride=8)) for h in range(2)], 0)
            qkv = dot(norm(first), wqkv[...]).astype(BF16)
            parts = []
            for grp in range(3):
                q, k, v = (qkv[:, C * a + 128 * grp : C * a + 128 * grp + 128] for a in range(3))
                v = jnp.concatenate([v, ones], 1)
                att = None
                for h in range(4):
                    mine = (lane >= h * HD) & (lane < (h + 1) * HD)
                    qh = jnp.where(mine, q.astype(F32), 0.0).astype(BF16)
                    sc = lax.dot_general(qh, k, (((1,), (1,)), ((), ())), preferred_element_type=F32)
                    sc = sc - jnp.max(sc, axis=-1, keepdims=True)
                    pv = dot(jnp.exp2(sc * expo).astype(BF16), v)
                    pv = pv[:, :128] / pv[:, 128:]
                    att = pv if att is None else jnp.where(mine, pv, att)
                parts.append(att.astype(BF16))
            second = first + flag * dot(jnp.concatenate(parts, 1), wo[...])
            second = second.astype(BF16).astype(F32)
            for h in range(2):
                put(t, pl.ds(2 * j + h, DEV, stride=8), second[h * DEV : (h + 1) * DEV])
            return 0

        lax.fori_loop(0, 4, window, 0)

        def mlp(gg, _):
            g = lax.rem(own_g + gg, 4)
            second = jnp.concatenate([take(t, pl.ds((i * 4 + g) * 64, 64)) for i in range(4)], 0)
            normed = norm(second)
            for n in range(0, EX, CH):
                mx[:, n : n + CH] = gelu(dot(normed, wi[:, n : n + CH])).astype(BF16)
            res = (second + flag_two * dot(mx[...], w2[...])).astype(BF16)
            for i in range(4):
                z[f, pl.ds((i * 4 + g) * WA, WA)] = res[i * 64 : (i + 1) * 64].reshape(8, 8, C)
            spread(z, o, z_send, z_recv, f, g, gg)
            return 0

        lax.fori_loop(0, 4, mlp, 0)
        o[f, me] = z[f, me]
        return 0

    lax.fori_loop(0, FR, attention, 0)

    def gather(f, _):
        arrived(z, o, z_send, z_recv, f).wait_recv()

        def row(y, _):
            h = lax.rem(y, 4) * 4 + y // 4
            put(fs, slice(0, 64), o[f, pl.ds(h * WA, WA)].astype(F32).reshape(64, C))
            for half in range(2):
                out[f, y, half * 32 : half * 32 + 32] = take(fs, pl.ds(half, 32, stride=2)).astype(BF16)
            return 0

        lax.fori_loop(0, RO, row, 0)
        return 0

    lax.fori_loop(0, FR, gather, 0)
    for f in range(FR):
        arrived(s, r, s_send, s_recv, f).wait_send()
        arrived(z, o, z_send, z_recv, f).wait_send()


def body(frames, keep, we, dwk, bias, wp, wqkv, wo, wi, w2):
    vmem = pl.BlockSpec(memory_space=pltpu.VMEM)
    dma = pltpu.SemaphoreType.DMA
    slots = pltpu.VMEM((FR, DEV, 8, C), BF16)
    return pl.pallas_call(
        kernel,
        out_shape=jax.ShapeDtypeStruct(frames.shape, BF16),
        in_specs=[vmem, pl.BlockSpec(memory_space=pltpu.SMEM)] + [vmem] * 8,
        out_specs=vmem,
        scratch_shapes=[
            pltpu.VMEM((FR, RO, CO, C), BF16),
            pltpu.VMEM((2, FR, RO, C), BF16),
            pltpu.VMEM((FR, 224, C), BF16),
            pltpu.VMEM((FR, RO + 2, 10, 8, EX), F32),
            pltpu.VMEM((10, 8, EX), F32),
            pltpu.VMEM((2, 48, EX), F32),
            pltpu.VMEM((256, EX), BF16),
            slots, slots, slots, slots,
            pltpu.VMEM((3, DEV * 8, 128), F32),
            pltpu.VMEM((3, 256, 128), F32),
            dma((FR, 8)), dma((FR, 8)), dma((FR,)), dma((FR,)), dma((FR,)), dma((FR,)),
            pltpu.SemaphoreType.REGULAR,
        ],
        compiler_params=pltpu.CompilerParams(
            collective_id=0, has_side_effects=True, vmem_limit_bytes=60 * 1024 * 1024
        ),
        name="block",
    )(frames, keep, we, dwk.reshape(9, EX), bias.reshape(1, EX), wp, wqkv, wo, wi, w2)


def solution(mesh):
    in_specs = (P(None, "ha", "wa", None), P(), P(), P(), P(), P(), P(), P(), P(), P())
    return jax.shard_map(body, mesh=mesh, in_specs=in_specs, out_specs=P(None, "ha", "wa", None), check_vma=False)
```

time: 217 us -> 84.5 us (0.39)
  matrix products: 88.8 us -> 0 us
  Pallas kernels: 0 us -> 78.7 us
  waiting for transfers between devices: 38.3 us -> 0 us
  blocking collectives: 29.2 us -> 0 us
  starting transfers between devices: 25.8 us -> 0 us
  local copies, waits for them, and re-layouts: 23.7 us -> 5.56 us
  other arithmetic: 10 us -> 0 us
    pallas_call x0 -> x1, Pallas kernels: none -> 78.7 us  [body(): pl.pallas_call(kernel, out_shape=jax.ShapeDtypeStruct(frames.shape, BF16)...]
    dot_general x15 -> x0, matrix products: 69.4 us -> none  [the longest x1 24.8 us: body(): branch = jnp.dot(mixed, project_weight, preferred_element_type=jnp.float32)]
    all_to_all x1 -> x0, blocking collectives: 29.2 us -> none  [body(): lax.all_to_all(flat_back, ('ha', 'wa'), split_axis=1, concat_axis=1, tile...]
    all_to_all x1 -> x0, waiting for transfers between devices: 24.4 us -> none  [body(): lax.all_to_all(flat_send, ('ha', 'wa'), split_axis=1, concat_axis=1, tile...]
    sub x4 -> x0, matrix products: 19.5 us -> none  [attend(): weights = jnp.exp(scores - top_score)]
    ppermute x4 -> x0, waiting for transfers between devices: 13.9 us -> none  [the longest x2 9.21 us: with_halo(): before = lax.ppermute(last, axis, up)]
    all_to_all x1 -> x0, starting transfers between devices: 13 us -> none  [body(): lax.all_to_all(flat_send, ('ha', 'wa'), split_axis=1, concat_axis=1, tile...]
    ppermute x4 -> x0, starting transfers between devices: 12.8 us -> none  [the longest x2 9.54 us: with_halo(): before = lax.ppermute(last, axis, up)]
  transfers between devices with their start and end apart: 5 -> 0, of which waited for: 5 -> 0; matrix products, arithmetic and copies ran while one was open for 0% -> 0% of each run, Pallas kernels for 0% -> 0%
where the time goes in v1:
time: 84.5 us; the launch traced here: 84.3 us
  Pallas kernels  78.7 us (93%)
  local copies, waits for them, and re-layouts  5.56 us (7%)
    pallas_call x1, Pallas kernels, body(): pl.pallas_call(kernel, out_shape=jax.ShapeDtypeStruct(frames.shape, BF16)...  78.7 us
    unnamed x1, local copies, waits for them, and re-layouts  2.72 us

profile of v1, /device:TPU:1, one launch (start us, length us, event | category | flops | bytes accessed | tf_op | source)
XLA Modules:
  0.0 84.3 jit_solution(10566439509467897608)
XLA Ops:
  0.0 1.3 %reshape.7.bias = f32[1,1536]{1,0:T(1,128)} reshape(f32[1536]{0:T(1024)} %param.14) | data formatting | bytes 12288 | tf_op jit(solution)/shard_map/reshape | solution.py:311
  1.3 1.6 %reshape.6.dwk = f32[9,1536]{1,0:T(8,128)} reshape(f32[3,3,1536]{2,1,0:T(4,128)} %param.13) | data formatting | bytes 110592 | tf_op jit(solution)/shard_map/reshape | solution.py:311
  2.8 78.7 %block.1 = bf16[2,16,64,384]{3,2,1,0:T(8,128)(2,1)} custom-call(bf16[2,16,64,384]{3,2,1,0:T(8,128)(2,1)} %x.1, s32[2,3]{1,0:T(2,128)} %keep.1, bf16[384,1536]{1,0:T(8,128)(2,1)} %we.1, f32[9,1536]{1,0:T(8,128)} %reshape.6.dwk, f32[1,1536]{1,0:T(1,128)} %reshape.7.bias, bf16[1536,384]{1,0:T(8,128)(2,1)} %wp.1, bf16[384,1152]{1,0:T(8,128)(2,1)} %wqkv.1, ...), custom_call_target="tpu_custom_call" | custom-call | tf_op jit(solution)/shard_map/block/pallas_call | solution.py:288
  81.5 2.7 %copy.12 = bf16[2,16,64,384]{3,2,1,0:T(8,128)(2,1)} copy(bf16[2,16,64,384]{3,2,1,0:T(8,128)(2,1)} %block.1) | data formatting | bytes 3145728

commit v2 on v1

v2 whole, which is shorter than its diff:
```python
import functools
import math

import jax
import jax.numpy as jnp
from jax import lax
from jax.experimental import pallas as pl
from jax.experimental.pallas import tpu as pltpu
from jax.sharding import PartitionSpec as P

MESH = pl.DeviceIdType.MESH
F32, BF16 = jnp.float32, jnp.bfloat16
HA, WA = 16, 8
DEV = HA * WA
FR, RO, CO, C, EX = 2, 16, 64, 384, 1536
HEADS, HD = 12, 32
CH = 256
GA, GB = math.sqrt(2 / math.pi), math.sqrt(2 / math.pi) * 0.044715


def gelu(v):
    half = 0.5 * v
    return half + half * jnp.tanh(v * (GA + GB * (v * v)))


def norm(v):
    c = v - jnp.mean(v, axis=-1, keepdims=True)
    return (c * lax.rsqrt(jnp.mean(c * c, axis=-1, keepdims=True) + 1e-05)).astype(BF16)


def put(ref, rows, value):
    for l in range(3):
        ref[l, rows, :] = value[:, 128 * l : 128 * l + 128]


def take(ref, rows):
    return jnp.concatenate([ref[l, rows, :] for l in range(3)], 1)


def dot(a, b):
    return jnp.dot(a, b, preferred_element_type=F32)


def kernel(
    x_hbm, keep, we_hbm, dwk_hbm, bias_hbm, wp_hbm, wqkv_hbm, wo_hbm, wi_hbm, w2_hbm, out,
    x, we, dwk, bias, wp, wqkv, wo, wi, w2,
    xp, cols, hb, e, kb, le, mx, s, r, z, t, fs,
    loads, halo_send, halo_recv, s_send, s_recv, z_send, z_recv, own, entry,
):
    ha, wa = lax.axis_index("ha"), lax.axis_index("wa")
    me = ha * WA + wa
    own_x, own_g = ha // 4, lax.rem(ha, 4)

    def at(h, w):
        return {"ha": h, "wa": w}

    barrier = pltpu.get_barrier_semaphore()
    near = [(ha, lax.rem(wa + i, WA)) for i in range(1, WA)]
    near += [(lax.rem(ha + i, HA), wa) for i in range(1, HA)]
    near += [(lax.rem(ha + i, HA), lax.rem(wa + j, WA)) for i in (1, HA - 1) for j in (1, WA - 1)]
    for h, w in near:
        pl.semaphore_signal(barrier, 1, device_id=at(h, w), device_id_type=MESH)

    arrays = (
        (x_hbm, x), (we_hbm, we), (dwk_hbm, dwk), (bias_hbm, bias), (wp_hbm, wp),
        (wqkv_hbm, wqkv), (wo_hbm, wo), (wi_hbm, wi), (w2_hbm, w2),
    )
    fetch = [pltpu.make_async_copy(src, dst, loads.at[i]) for i, (src, dst) in enumerate(arrays)]
    for c in fetch:
        c.start()
    fetch[0].wait()

    def permute(f, _):
        put(t, slice(None), x[f].astype(F32).reshape(RO * CO, C))

        def one(row, _):
            for q in range(4):
                xp[f, row, q * 16 : q * 16 + 16, :] = take(t, pl.ds(row * CO + q, 16, stride=4)).astype(BF16)
            return 0

        lax.fori_loop(0, RO, one, 0)
        for side in range(2):
            cols[side, f] = take(t, pl.ds(side * (CO - 1), RO, stride=CO)).astype(BF16)
        return 0

    lax.fori_loop(0, FR, permute, 0)

    def expand(f, _):
        def rows(q, _):
            tokens = xp[f, pl.ds(q * 4, 4)].reshape(256, C)
            for n in range(0, EX, CH):
                v = gelu(dot(tokens, we[:, n : n + CH]).astype(BF16))
                e[f, pl.ds(q * 4 + 1, 4), 1:5, :, n : n + CH] = v.reshape(4, 4, 16, CH)
            return 0

        return lax.fori_loop(0, 4, rows, 0)

    pl.semaphore_wait(barrier, len(near))
    for h, w in near[: WA - 1]:
        pl.semaphore_signal(entry, 1, device_id=at(h, w), device_id_type=MESH)

    up, down = lax.rem(ha + HA - 1, HA), lax.rem(ha + 1, HA)
    left, right = lax.rem(wa + WA - 1, WA), lax.rem(wa + 1, WA)

    def halo(f):
        moves = [
            (xp.at[f, RO - 1], hb.at[f, 0:64], (down, wa)),
            (xp.at[f, 0], hb.at[f, 64:128], (up, wa)),
        ]
        for side, w in ((1, right), (0, left)):
            for blk, h in ((0, down), (1, ha), (2, up)):
                first = 128 + (1 - side) * 48 + blk * 16
                moves.append((cols.at[side, f], hb.at[f, first : first + 16], (h, w)))
        return [
            pltpu.make_async_remote_copy(
                src, dst, halo_send.at[f, i], halo_recv.at[f, i], device_id=at(*to), device_id_type=MESH
            )
            for i, (src, dst, to) in enumerate(moves)
        ]

    halos = [halo(f) for f in range(FR)]
    for f in range(FR):
        for c in halos[f]:
            c.start()
    fetch[1].wait()
    expand(0, 0)
    for c in fetch[2:]:
        c.wait()
    for i in range(3):
        for j in range(3):
            kb[3 * i + j] = jnp.broadcast_to(dwk[i, j : j + 1, :], (16, EX)).astype(BF16)
    kb[9] = jnp.broadcast_to(bias[...].reshape(1, EX), (16, EX)).astype(BF16)
    ok_up, ok_down = (ha > 0).astype(F32), (ha < HA - 1).astype(F32)
    ok_side = ((wa > 0).astype(F32), (wa < WA - 1).astype(F32))
    sub = lax.broadcasted_iota(jnp.int32, (16, EX), 0)

    def edges(f, _):
        tokens = hb[f]
        for n in range(0, EX, CH):
            v = gelu(dot(tokens, we[:, n : n + CH]))
            e[f, 0, 1:5, :, n : n + CH] = (v[0:64] * ok_up).astype(BF16).reshape(4, 16, CH)
            e[f, RO + 1, 1:5, :, n : n + CH] = (v[64:128] * ok_down).astype(BF16).reshape(4, 16, CH)
            for side in range(2):
                p = 128 + side * 48
                le[side, 0:16, n : n + CH] = v[p : p + 16] * (ok_side[side] * ok_up)
                le[side, 16:32, n : n + CH] = v[p + 16 : p + 32] * ok_side[side]
                le[side, 32:48, n : n + CH] = v[p + 32 : p + 48] * (ok_side[side] * ok_down)

        def fill(p, _):
            for side, (inner, outer, turn, edge) in enumerate(((4, 0, 1, 0), (1, 5, 15, 15))):
                moved = pltpu.roll(e[f, p, inner].astype(F32), turn, 0)
                beyond = jnp.broadcast_to(le[side, pl.ds(15 + p, 1), :], (16, EX))
                e[f, p, outer] = jnp.where(sub == edge, beyond, moved).astype(BF16)
            return 0

        lax.fori_loop(0, RO + 2, fill, 0)
        return 0


    def partner(i, g, k):
        h, w = lax.rem(own_x + i, 4) * 4 + g, lax.rem(wa + k, WA)
        return h, w

    def spread(src, dst, send, recv, f, gg, i):
        g = lax.rem(own_g + gg, 4)
        for k in range(8):
            if gg + i + k > 0:
                h, w = partner(i, g, k)
                pltpu.make_async_remote_copy(
                    src.at[f, h * WA + w], dst.at[f, me], send.at[f], recv.at[f],
                    device_id=at(h, w), device_id_type=MESH,
                ).start()

    def arrived(src, dst, send, recv, f):
        return pltpu.make_async_remote_copy(
            src.at[f, 0 : DEV - 1], dst.at[f, 0 : DEV - 1], send.at[f], recv.at[f],
            device_id=at(ha, wa), device_id_type=MESH,
        )

    pl.semaphore_wait(entry, WA - 1)

    def conv(f, _):
        flag = keep[f, 0].astype(F32)

        def row(gg, rr):
            y = lax.rem(own_g + gg, 4) * 4 + rr
            for n in range(0, EX, 128):
                sums = []
                for i in range(3):
                    taps = [e[f, y + i, j : j + 4, :, n : n + 128] * kb[3 * i + j, :, n : n + 128][None] for j in range(3)]
                    sums.append(taps[0] + taps[1] + taps[2])
                acc = (sums[0] + sums[1]) + (sums[2] + kb[9, :, n : n + 128][None])
                mx[gg % 2, rr * 64 : rr * 64 + 64, n : n + 128] = gelu(acc).reshape(64, 128)

        def project(gg):
            g = lax.rem(own_g + gg, 4)
            tokens = xp[f, pl.ds(g * 4, 4)].reshape(256, C)
            put(fs, slice(None), tokens.astype(F32) + flag * dot(mx[gg % 2], wp[...]))
            for i in range(4):
                for k in range(8):
                    part = take(fs, pl.ds(i * 64 + k, 8, stride=8))
                    s[f, (i * 4 + g) * WA + k] = part.astype(BF16)

        for gg in range(5):
            if gg > 0:
                project(gg - 1)
            for rr in range(4):
                if gg < 4:
                    row(gg, rr)
                if gg > 0:
                    spread(s, r, s_send, s_recv, f, gg - 1, rr)
        r[f, me] = s[f, me]
        return 0

    def front(f, _):
        @pl.when(f > 0)
        def _():
            expand(f, 0)

        for c in halo(f):
            c.wait()
        edges(f, 0)
        return conv(f, 0)

    lax.fori_loop(0, FR, front, 0)

    lane = lax.broadcasted_iota(jnp.int32, (256, 128), 1)
    heads = [(lane >= h * HD) & (lane < (h + 1) * HD) for h in range(4)]
    masks = [m.astype(F32).astype(BF16) for m in heads]
    ones = jnp.ones((256, 128), BF16)
    expo = HD**-0.5 * math.log2(math.e)

    def attention(f, _):
        arrived(s, r, s_send, s_recv, f).wait_recv()
        put(t, slice(None), r[f].astype(F32).reshape(DEV * 8, C))
        flag, flag_two = keep[f, 1].astype(F32), keep[f, 2].astype(F32)

        def window(j, _):
            first = jnp.concatenate([take(t, pl.ds(2 * j + h, DEV, stride=8)) for h in range(2)], 0)
            qkv = dot(norm(first), wqkv[...]).astype(BF16)
            parts = []
            for grp in range(3):
                q, k, v = (qkv[:, C * a + 128 * grp : C * a + 128 * grp + 128] for a in range(3))
                v = jnp.concatenate([v, ones], 1)
                att = None
                for h in range(4):
                    sc = lax.dot_general(q * masks[h], k, (((1,), (1,)), ((), ())), preferred_element_type=F32)
                    sc = sc - jnp.max(sc, axis=-1, keepdims=True)
                    pv = dot(jnp.exp2(sc * expo).astype(BF16), v)
                    pv = pv[:, :128] / pv[:, 128:]
                    att = pv if att is None else jnp.where(heads[h], pv, att)
                parts.append(att.astype(BF16))
            second = first + flag * dot(jnp.concatenate(parts, 1), wo[...])
            second = second.astype(BF16).astype(F32)
            for h in range(2):
                put(t, pl.ds(2 * j + h, DEV, stride=8), second[h * DEV : (h + 1) * DEV])
            return 0

        lax.fori_loop(0, 4, window, 0)

        def mlp(gg):
            g = lax.rem(own_g + gg, 4)
            second = jnp.concatenate([take(t, pl.ds((i * 4 + g) * 64, 64)) for i in range(4)], 0)
            normed = norm(second)
            for n in range(0, EX, CH):
                mx[gg % 2, :, n : n + CH] = gelu(dot(normed, wi[:, n : n + CH]).astype(BF16))
            res = (second + flag_two * dot(mx[gg % 2], w2[...])).astype(BF16)
            for i in range(4):
                z[f, pl.ds((i * 4 + g) * WA, WA)] = res[i * 64 : (i + 1) * 64].reshape(8, 8, C)

        for gg in range(5):
            if gg > 0:
                for i in range(4):
                    spread(z, out, z_send, z_recv, f, gg - 1, i)
            if gg < 4:
                mlp(gg)
        pltpu.make_async_copy(z.at[f, me], out.at[f, me], own.at[f]).start()
        return 0

    lax.fori_loop(0, FR, attention, 0)

    for f in range(FR):
        pltpu.make_async_copy(z.at[f, me], out.at[f, me], own.at[f]).wait()
        arrived(z, out, z_send, z_recv, f).wait_recv()
    for f in range(FR):
        arrived(s, r, s_send, s_recv, f).wait_send()
        arrived(z, out, z_send, z_recv, f).wait_send()


def gather(o, out, fs):
    for g in range(o.shape[2]):
        for i in range(4):
            n = 4 * g + i
            put(fs, slice(64 * n, 64 * n + 64), o[0, i, g].astype(F32).reshape(64, C))
            for half in range(2):
                part = take(fs, pl.ds(64 * n + half, 32, stride=2))
                out[0, n, half * 32 : half * 32 + 32] = part.astype(BF16)


def body(frames, keep, we, dwk, bias, wp, wqkv, wo, wi, w2):
    hbm = pl.BlockSpec(memory_space=pl.ANY)
    dma = pltpu.SemaphoreType.DMA
    slots = pltpu.VMEM((FR, DEV, 8, C), BF16)
    arrays = (frames, we, dwk, bias, wp, wqkv, wo, wi, w2)
    result = pl.pallas_call(
        kernel,
        out_shape=jax.ShapeDtypeStruct((FR, DEV, 8, C), BF16),
        in_specs=[hbm, pl.BlockSpec(memory_space=pltpu.SMEM)] + [hbm] * 8,
        out_specs=hbm,
        scratch_shapes=[pltpu.VMEM(a.shape, a.dtype) for a in arrays] + [
            pltpu.VMEM((FR, RO, CO, C), BF16),
            pltpu.VMEM((2, FR, RO, C), BF16),
            pltpu.VMEM((FR, 224, C), BF16),
            pltpu.VMEM((FR, RO + 2, 6, 16, EX), BF16),
            pltpu.VMEM((10, 16, EX), BF16),
            pltpu.VMEM((2, 48, EX), F32),
            pltpu.VMEM((2, 256, EX), BF16),
            slots, slots, slots,
            pltpu.VMEM((3, DEV * 8, 128), F32),
            pltpu.VMEM((3, 256, 128), F32),
            dma((len(arrays),)), dma((FR, 8)), dma((FR, 8)),
            dma((FR,)), dma((FR,)), dma((FR,)), dma((FR,)), dma((FR,)),
            pltpu.SemaphoreType.REGULAR,
        ],
        compiler_params=pltpu.CompilerParams(
            collective_id=0, has_side_effects=True, vmem_limit_bytes=60 * 1024 * 1024
        ),
        name="block",
    )(frames, keep, we, dwk, bias, wp, wqkv, wo, wi, w2)
    steps = 2
    return pl.pallas_call(
        gather,
        out_shape=jax.ShapeDtypeStruct(frames.shape, BF16),
        grid=(FR, steps),
        in_specs=[pl.BlockSpec((1, 4, 4 // steps, 8, 8, C), lambda f, g: (f, 0, g, 0, 0, 0))],
        out_specs=pl.BlockSpec((1, RO // steps, CO, C), lambda f, g: (f, g, 0, 0)),
        scratch_shapes=[pltpu.VMEM((3, RO // steps * CO, 128), F32)],
        name="rows",
    )(result.reshape(FR, 4, 4, 8, 8, C))


def solution(mesh):
    in_specs = (P(None, "ha", "wa", None), P(), P(), P(), P(), P(), P(), P(), P(), P())
    return jax.shard_map(body, mesh=mesh, in_specs=in_specs, out_specs=P(None, "ha", "wa", None), check_vma=False)
```

time: 84.5 us -> 78.2 us (0.925)
  local copies, waits for them, and re-layouts: 5.56 us -> 0 us
    reshape x2 -> x0, local copies, waits for them, and re-layouts: 2.84 us -> none  [the longest x1 1.55 us: body(): dwk.reshape(9, EX)]
    unnamed x1 -> x0, local copies, waits for them, and re-layouts: 2.72 us -> none
    pallas_call x1 -> x2, Pallas kernels: 78.7 us -> 78 us  [the longest x1 74.2 us: body(): pl.pallas_call(kernel, out_shape=jax.ShapeDtypeStruct((FR, DEV, 8, C), BF...]
where the time goes in v2:
time: 78.2 us; the launch traced here: 78 us
  Pallas kernels  78 us (100%)
    pallas_call x1, Pallas kernels, body(): pl.pallas_call(kernel, out_shape=jax.ShapeDtypeStruct((FR, DEV, 8, C), BF...  74.2 us
    pallas_call x1, Pallas kernels, body(): pl.pallas_call(gather, out_shape=jax.ShapeDtypeStruct(frames.shape, BF16)...  3.77 us

profile of v2, /device:TPU:1, one launch (start us, length us, event | category | flops | bytes accessed | tf_op | source)
XLA Modules:
  0.0 78.0 jit_solution(6270505886199705157)
XLA Ops:
  0.0 74.2 %block.1 = bf16[2,128,8,384]{3,2,1,0:T(8,128)(2,1)} custom-call(bf16[2,16,64,384]{3,2,1,0:T(8,128)(2,1)} %x_hbm.1, s32[2,3]{1,0:T(2,128)} %keep.1, bf16[384,1536]{1,0:T(8,128)(2,1)} %we_hbm.1, f32[3,3,1536]{2,1,0:T(4,128)} %dwk_hbm.1, f32[1536]{0:T(1024)} %bias_hbm.1, bf16[1536,384]{1,0:T(8,128)(2,1)} %wp_hbm.1, bf16[384,1152]{1,0:T(8,128)(2,1)} %wqkv_hbm.1, ...), custom_call_target="tpu_custom_call" | custom-call | tf_op jit(solution)/shard_map/block/pallas_call | solution.py:305
  74.2 3.8 %rows.1 = bf16[2,16,64,384]{3,2,1,0:T(8,128)(2,1)} custom-call(bf16[2,4,4,8,8,384]{5,4,3,2,1,0:T(8,128)(2,1)} %bitcast.1), custom_call_target="tpu_custom_call" | custom-call | tf_op jit(solution)/shard_map/rows/pallas_call | solution.py:331

commit v3 on v2

--- a/solution.py
+++ b/solution.py
@@ -14,6 +14,7 @@
 DEV = HA * WA
 FR, RO, CO, C, EX = 2, 16, 64, 384, 1536
 HEADS, HD = 12, 32
+UNROLL = 2
 CH = 256
 GA, GB = math.sqrt(2 / math.pi), math.sqrt(2 / math.pi) * 0.044715
 
@@ -23,6 +24,10 @@
     return half + half * jnp.tanh(v * (GA + GB * (v * v)))
 
 
+def gelu_of_half(half):
+    return half + half * jnp.tanh(half * (2 * GA + 8 * GB * (half * half)))
+
+
 def norm(v):
     c = v - jnp.mean(v, axis=-1, keepdims=True)
     return (c * lax.rsqrt(jnp.mean(c * c, axis=-1, keepdims=True) + 1e-05)).astype(BF16)
@@ -44,7 +49,7 @@
 def kernel(
     x_hbm, keep, we_hbm, dwk_hbm, bias_hbm, wp_hbm, wqkv_hbm, wo_hbm, wi_hbm, w2_hbm, out,
     x, we, dwk, bias, wp, wqkv, wo, wi, w2,
-    xp, cols, hb, e, kb, le, mx, s, r, z, t, fs,
+    xp, cols, hb, e, kb, le, mx, s, r, z, o, t, fs,
     loads, halo_send, halo_recv, s_send, s_recv, z_send, z_recv, own, entry,
 ):
     ha, wa = lax.axis_index("ha"), lax.axis_index("wa")
@@ -128,8 +133,8 @@
         c.wait()
     for i in range(3):
         for j in range(3):
-            kb[3 * i + j] = jnp.broadcast_to(dwk[i, j : j + 1, :], (16, EX)).astype(BF16)
-    kb[9] = jnp.broadcast_to(bias[...].reshape(1, EX), (16, EX)).astype(BF16)
+            kb[3 * i + j] = jnp.broadcast_to(0.5 * dwk[i, j : j + 1, :], (16, EX))
+    kb[9] = jnp.broadcast_to(0.5 * bias[...].reshape(1, EX), (16, EX))
     ok_up, ok_down = (ha > 0).astype(F32), (ha < HA - 1).astype(F32)
     ok_side = ((wa > 0).astype(F32), (wa < WA - 1).astype(F32))
     sub = lax.broadcasted_iota(jnp.int32, (16, EX), 0)
@@ -137,11 +142,12 @@
     def edges(f, _):
         tokens = hb[f]
         for n in range(0, EX, CH):
-            v = gelu(dot(tokens, we[:, n : n + CH]))
-            e[f, 0, 1:5, :, n : n + CH] = (v[0:64] * ok_up).astype(BF16).reshape(4, 16, CH)
-            e[f, RO + 1, 1:5, :, n : n + CH] = (v[64:128] * ok_down).astype(BF16).reshape(4, 16, CH)
+            v = gelu(dot(tokens, we[:, n : n + CH]).astype(BF16))
+            e[f, 0, 1:5, :, n : n + CH] = (v[0:64] * ok_up.astype(BF16)).reshape(4, 16, CH)
+            e[f, RO + 1, 1:5, :, n : n + CH] = (v[64:128] * ok_down.astype(BF16)).reshape(4, 16, CH)
+            v = v[128:].astype(F32)
             for side in range(2):
-                p = 128 + side * 48
+                p = side * 48
                 le[side, 0:16, n : n + CH] = v[p : p + 16] * (ok_side[side] * ok_up)
                 le[side, 16:32, n : n + CH] = v[p + 16 : p + 32] * ok_side[side]
                 le[side, 32:48, n : n + CH] = v[p + 32 : p + 48] * (ok_side[side] * ok_down)
@@ -161,20 +167,22 @@
         h, w = lax.rem(own_x + i, 4) * 4 + g, lax.rem(wa + k, WA)
         return h, w
 
-    def spread(src, dst, send, recv, f, gg, i):
+    def spread(src, dst, send, recv, gg):
         g = lax.rem(own_g + gg, 4)
-        for k in range(8):
-            if gg + i + k > 0:
+        for i in range(4):
+            for k in range(8):
                 h, w = partner(i, g, k)
-                pltpu.make_async_remote_copy(
-                    src.at[f, h * WA + w], dst.at[f, me], send.at[f], recv.at[f],
-                    device_id=at(h, w), device_id_type=MESH,
-                ).start()
-
-    def arrived(src, dst, send, recv, f):
+                copy = pltpu.make_async_remote_copy(
+                    src.at[h * WA + w], dst.at[me], send, recv, device_id=at(h, w), device_id_type=MESH
+                )
+                if i + k > 0:
+                    copy.start()
+                else:
+                    pl.when(gg > 0)(copy.start)
+
+    def arrived(src, dst, send, recv):
         return pltpu.make_async_remote_copy(
-            src.at[f, 0 : DEV - 1], dst.at[f, 0 : DEV - 1], send.at[f], recv.at[f],
-            device_id=at(ha, wa), device_id_type=MESH,
+            src.at[0 : DEV - 1], dst.at[0 : DEV - 1], send, recv, device_id=at(ha, wa), device_id_type=MESH
         )
 
     pl.semaphore_wait(entry, WA - 1)
@@ -182,33 +190,28 @@
     def conv(f, _):
         flag = keep[f, 0].astype(F32)
 
-        def row(gg, rr):
-            y = lax.rem(own_g + gg, 4) * 4 + rr
-            for n in range(0, EX, 128):
-                sums = []
-                for i in range(3):
-                    taps = [e[f, y + i, j : j + 4, :, n : n + 128] * kb[3 * i + j, :, n : n + 128][None] for j in range(3)]
-                    sums.append(taps[0] + taps[1] + taps[2])
-                acc = (sums[0] + sums[1]) + (sums[2] + kb[9, :, n : n + 128][None])
-                mx[gg % 2, rr * 64 : rr * 64 + 64, n : n + 128] = gelu(acc).reshape(64, 128)
-
-        def project(gg):
+        def group(gg, _):
             g = lax.rem(own_g + gg, 4)
+            for rr in range(0, 4, 2):
+                for n in range(0, EX, 128):
+                    taps = [kb[i, :, n : n + 128].astype(BF16)[None] for i in range(10)]
+                    for q in range(rr, rr + 2):
+                        sums = []
+                        for i in range(3):
+                            part = [taps[3 * i + j] * e[f, g * 4 + q + i, j : j + 4, :, n : n + 128] for j in range(3)]
+                            sums.append(part[0] + part[1] + part[2])
+                        acc = (sums[0] + sums[1]) + (sums[2] + taps[9])
+                        mx[q * 64 : q * 64 + 64, n : n + 128] = gelu_of_half(acc).reshape(64, 128)
             tokens = xp[f, pl.ds(g * 4, 4)].reshape(256, C)
-            put(fs, slice(None), tokens.astype(F32) + flag * dot(mx[gg % 2], wp[...]))
+            put(fs, slice(None), tokens.astype(F32) + flag * dot(mx[...], wp[...]))
             for i in range(4):
                 for k in range(8):
                     part = take(fs, pl.ds(i * 64 + k, 8, stride=8))
                     s[f, (i * 4 + g) * WA + k] = part.astype(BF16)
-
-        for gg in range(5):
-            if gg > 0:
-                project(gg - 1)
-            for rr in range(4):
-                if gg < 4:
-                    row(gg, rr)
-                if gg > 0:
-                    spread(s, r, s_send, s_recv, f, gg - 1, rr)
+            spread(s.at[f], r.at[f], s_send.at[f], s_recv.at[f], gg)
+            return 0
+
+        lax.fori_loop(0, 4, group, 0)
         r[f, me] = s[f, me]
         return 0
 
@@ -230,10 +233,16 @@
     ones = jnp.ones((256, 128), BF16)
     expo = HD**-0.5 * math.log2(math.e)
 
+    def mlp(second, flag):
+        normed = norm(second)
+        for n in range(0, EX, CH):
+            mx[:, n : n + CH] = gelu(dot(normed, wi[:, n : n + CH]).astype(BF16))
+        return (second + flag * dot(mx[...], w2[...])).astype(BF16)
+
     def attention(f, _):
-        arrived(s, r, s_send, s_recv, f).wait_recv()
+        arrived(s.at[f], r.at[f], s_send.at[f], s_recv.at[f]).wait_recv()
         put(t, slice(None), r[f].astype(F32).reshape(DEV * 8, C))
-        flag, flag_two = keep[f, 1].astype(F32), keep[f, 2].astype(F32)
+        flag = keep[f, 1].astype(F32)
 
         def window(j, _):
             first = jnp.concatenate([take(t, pl.ds(2 * j + h, DEV, stride=8)) for h in range(2)], 0)
@@ -256,35 +265,58 @@
                 put(t, pl.ds(2 * j + h, DEV, stride=8), second[h * DEV : (h + 1) * DEV])
             return 0
 
-        lax.fori_loop(0, 4, window, 0)
-
-        def mlp(gg):
-            g = lax.rem(own_g + gg, 4)
-            second = jnp.concatenate([take(t, pl.ds((i * 4 + g) * 64, 64)) for i in range(4)], 0)
-            normed = norm(second)
-            for n in range(0, EX, CH):
-                mx[gg % 2, :, n : n + CH] = gelu(dot(normed, wi[:, n : n + CH]).astype(BF16))
-            res = (second + flag_two * dot(mx[gg % 2], w2[...])).astype(BF16)
-            for i in range(4):
-                z[f, pl.ds((i * 4 + g) * WA, WA)] = res[i * 64 : (i + 1) * 64].reshape(8, 8, C)
-
-        for gg in range(5):
-            if gg > 0:
+        def windows(p, _):
+            for u in range(UNROLL):
+                window(p * UNROLL + u, 0)
+            return 0
+
+        lax.fori_loop(0, 4 // UNROLL, windows, 0)
+
+        @pl.when(f == 0)
+        def _():
+            z[0] = take(t, slice(None)).astype(BF16).reshape(DEV, 8, C)
+
+            def send(gg, _):
+                spread(z.at[0], o, z_send.at[0], z_recv.at[0], gg)
+                return 0
+
+            lax.fori_loop(0, 4, send, 0)
+            o[me] = z[0, me]
+
+        @pl.when(f == 1)
+        def _():
+            def block(gg, _):
+                g = lax.rem(own_g + gg, 4)
+                second = jnp.concatenate([take(t, pl.ds((i * 4 + g) * 64, 64)) for i in range(4)], 0)
+                res = mlp(second, keep[1, 2].astype(F32))
                 for i in range(4):
-                    spread(z, out, z_send, z_recv, f, gg - 1, i)
-            if gg < 4:
-                mlp(gg)
-        pltpu.make_async_copy(z.at[f, me], out.at[f, me], own.at[f]).start()
+                    z[1, pl.ds((i * 4 + g) * WA, WA)] = res[i * 64 : (i + 1) * 64].reshape(8, 8, C)
+                spread(z.at[1], out.at[1], z_send.at[1], z_recv.at[1], gg)
+                return 0
+
+            lax.fori_loop(0, 4, block, 0)
+            pltpu.make_async_copy(z.at[1, me], out.at[1, me], own.at[1]).start()
+
         return 0
 
     lax.fori_loop(0, FR, attention, 0)
-
+    arrived(z.at[0], o, z_send.at[0], z_recv.at[0]).wait_recv()
+
+    def home(b, _):
+        part = pl.ds(b * 32, 32)
+        second = o[part].astype(F32).reshape(256, C)
+        r[0, part] = mlp(second, keep[0, 2].astype(F32)).reshape(32, 8, C)
+        pltpu.make_async_copy(r.at[0, part], out.at[0, part], own.at[0]).start()
+        return 0
+
+    lax.fori_loop(0, 4, home, 0)
+    pltpu.make_async_copy(r.at[0], out.at[0], own.at[0]).wait()
+    pltpu.make_async_copy(z.at[1, me], out.at[1, me], own.at[1]).wait()
+    arrived(z.at[1], out.at[1], z_send.at[1], z_recv.at[1]).wait_recv()
+    arrived(z.at[1], out.at[1], z_send.at[1], z_recv.at[1]).wait_send()
+    arrived(z.at[0], o, z_send.at[0], z_recv.at[0]).wait_send()
     for f in range(FR):
-        pltpu.make_async_copy(z.at[f, me], out.at[f, me], own.at[f]).wait()
-        arrived(z, out, z_send, z_recv, f).wait_recv()
-    for f in range(FR):
-        arrived(s, r, s_send, s_recv, f).wait_send()
-        arrived(z, out, z_send, z_recv, f).wait_send()
+        arrived(s.at[f], r.at[f], s_send.at[f], s_recv.at[f]).wait_send()
 
 
 def gather(o, out, fs):
@@ -312,10 +344,11 @@
             pltpu.VMEM((2, FR, RO, C), BF16),
             pltpu.VMEM((FR, 224, C), BF16),
             pltpu.VMEM((FR, RO + 2, 6, 16, EX), BF16),
-            pltpu.VMEM((10, 16, EX), BF16),
+            pltpu.VMEM((10, 16, EX), F32),
             pltpu.VMEM((2, 48, EX), F32),
-            pltpu.VMEM((2, 256, EX), BF16),
+            pltpu.VMEM((256, EX), BF16),
             slots, slots, slots,
+            pltpu.VMEM((DEV, 8, C), BF16),
             pltpu.VMEM((3, DEV * 8, 128), F32),
             pltpu.VMEM((3, 256, 128), F32),
             dma((len(arrays),)), dma((FR, 8)), dma((FR, 8)),

time: 78.2 us -> 66.2 us (0.85)
  Pallas kernels: 78 us -> 66.1 us
    pallas_call x1, Pallas kernels: 74.2 us -> 62.3 us  [body(): pl.pallas_call(kernel, out_shape=jax.ShapeDtypeStruct((FR, DEV, 8, C), BF...]
where the time goes in v3:
time: 66.2 us; the launch traced here: 66.1 us
  Pallas kernels  66.1 us (100%)
    pallas_call x1, Pallas kernels, body(): pl.pallas_call(kernel, out_shape=jax.ShapeDtypeStruct((FR, DEV, 8, C), BF...  62.3 us
    pallas_call x1, Pallas kernels, body(): pl.pallas_call(gather, out_shape=jax.ShapeDtypeStruct(frames.shape, BF16)...  3.77 us

profile of v3, /device:TPU:1, one launch (start us, length us, event | category | flops | bytes accessed | tf_op | source)
XLA Modules:
  0.0 66.1 jit_solution(2820647839181408352)
XLA Ops:
  0.0 62.3 %block.1 = bf16[2,128,8,384]{3,2,1,0:T(8,128)(2,1)} custom-call(bf16[2,16,64,384]{3,2,1,0:T(8,128)(2,1)} %x_hbm.1, s32[2,3]{1,0:T(2,128)} %keep.1, bf16[384,1536]{1,0:T(8,128)(2,1)} %we_hbm.1, f32[3,3,1536]{2,1,0:T(4,128)} %dwk_hbm.1, f32[1536]{0:T(1024)} %bias_hbm.1, bf16[1536,384]{1,0:T(8,128)(2,1)} %wp_hbm.1, bf16[384,1152]{1,0:T(8,128)(2,1)} %wqkv_hbm.1, ...), custom_call_target="tpu_custom_call" | custom-call | tf_op jit(solution)/shard_map/block/pallas_call | solution.py:337
  62.3 3.8 %rows.1 = bf16[2,16,64,384]{3,2,1,0:T(8,128)(2,1)} custom-call(bf16[2,4,4,8,8,384]{5,4,3,2,1,0:T(8,128)(2,1)} %bitcast.1), custom_call_target="tpu_custom_call" | custom-call | tf_op jit(solution)/shard_map/rows/pallas_call | solution.py:364

commit v4 on v3

--- a/solution.py
+++ b/solution.py
@@ -49,12 +49,13 @@
 def kernel(
     x_hbm, keep, we_hbm, dwk_hbm, bias_hbm, wp_hbm, wqkv_hbm, wo_hbm, wi_hbm, w2_hbm, out,
     x, we, dwk, bias, wp, wqkv, wo, wi, w2,
-    xp, cols, hb, e, kb, le, mx, s, r, z, o, t, fs,
+    xp, cols, hb, e_first, e_second, kb, le, mx, s, r, z, o, t, fs,
     loads, halo_send, halo_recv, s_send, s_recv, z_send, z_recv, own, entry,
 ):
     ha, wa = lax.axis_index("ha"), lax.axis_index("wa")
     me = ha * WA + wa
     own_x, own_g = ha // 4, lax.rem(ha, 4)
+    e = (e_first, e_second)
 
     def at(h, w):
         return {"ha": h, "wa": w}
@@ -67,15 +68,14 @@
         pl.semaphore_signal(barrier, 1, device_id=at(h, w), device_id_type=MESH)
 
     arrays = (
-        (x_hbm, x), (we_hbm, we), (dwk_hbm, dwk), (bias_hbm, bias), (wp_hbm, wp),
+        (x_hbm.at[0], x.at[0]), (x_hbm.at[1], x.at[1]), (we_hbm, we), (dwk_hbm, dwk), (bias_hbm, bias), (wp_hbm, wp),
         (wqkv_hbm, wqkv), (wo_hbm, wo), (wi_hbm, wi), (w2_hbm, w2),
     )
     fetch = [pltpu.make_async_copy(src, dst, loads.at[i]) for i, (src, dst) in enumerate(arrays)]
     for c in fetch:
         c.start()
-    fetch[0].wait()
-
-    def permute(f, _):
+
+    def permute(f):
         put(t, slice(None), x[f].astype(F32).reshape(RO * CO, C))
 
         def one(row, _):
@@ -86,23 +86,12 @@
         lax.fori_loop(0, RO, one, 0)
         for side in range(2):
             cols[side, f] = take(t, pl.ds(side * (CO - 1), RO, stride=CO)).astype(BF16)
-        return 0
-
-    lax.fori_loop(0, FR, permute, 0)
-
-    def expand(f, _):
-        def rows(q, _):
-            tokens = xp[f, pl.ds(q * 4, 4)].reshape(256, C)
-            for n in range(0, EX, CH):
-                v = gelu(dot(tokens, we[:, n : n + CH]).astype(BF16))
-                e[f, pl.ds(q * 4 + 1, 4), 1:5, :, n : n + CH] = v.reshape(4, 4, 16, CH)
-            return 0
-
-        return lax.fori_loop(0, 4, rows, 0)
-
-    pl.semaphore_wait(barrier, len(near))
-    for h, w in near[: WA - 1]:
-        pl.semaphore_signal(entry, 1, device_id=at(h, w), device_id_type=MESH)
+
+    def expand(f, first, count):
+        tokens = xp[f, pl.ds(first, count)].reshape(count * 64, C)
+        for n in range(0, EX, CH):
+            v = gelu(dot(tokens, we[:, n : n + CH]).astype(BF16))
+            e[f][pl.ds(first + 1, count), 1:5, :, n : n + CH] = v.reshape(count, 4, 16, CH)
 
     up, down = lax.rem(ha + HA - 1, HA), lax.rem(ha + 1, HA)
     left, right = lax.rem(wa + WA - 1, WA), lax.rem(wa + 1, WA)
@@ -123,13 +112,19 @@
             for i, (src, dst, to) in enumerate(moves)
         ]
 
-    halos = [halo(f) for f in range(FR)]
     for f in range(FR):
-        for c in halos[f]:
+        fetch[f].wait()
+        permute(f)
+        if f == 0:
+            pl.semaphore_wait(barrier, len(near))
+            for h, w in near[: WA - 1]:
+                pl.semaphore_signal(entry, 1, device_id=at(h, w), device_id_type=MESH)
+        for c in halo(f):
             c.start()
-    fetch[1].wait()
-    expand(0, 0)
-    for c in fetch[2:]:
+    fetch[2].wait()
+    for q in range(2):
+        expand(0, q * 8, 8)
+    for c in fetch[3:]:
         c.wait()
     for i in range(3):
         for j in range(3):
@@ -139,12 +134,12 @@
     ok_side = ((wa > 0).astype(F32), (wa < WA - 1).astype(F32))
     sub = lax.broadcasted_iota(jnp.int32, (16, EX), 0)
 
-    def edges(f, _):
+    def edges(f):
         tokens = hb[f]
         for n in range(0, EX, CH):
             v = gelu(dot(tokens, we[:, n : n + CH]).astype(BF16))
-            e[f, 0, 1:5, :, n : n + CH] = (v[0:64] * ok_up.astype(BF16)).reshape(4, 16, CH)
-            e[f, RO + 1, 1:5, :, n : n + CH] = (v[64:128] * ok_down.astype(BF16)).reshape(4, 16, CH)
+            e[f][0, 1:5, :, n : n + CH] = (v[0:64] * ok_up.astype(BF16)).reshape(4, 16, CH)
+            e[f][RO + 1, 1:5, :, n : n + CH] = (v[64:128] * ok_down.astype(BF16)).reshape(4, 16, CH)
             v = v[128:].astype(F32)
             for side in range(2):
                 p = side * 48
@@ -154,13 +149,12 @@
 
         def fill(p, _):
             for side, (inner, outer, turn, edge) in enumerate(((4, 0, 1, 0), (1, 5, 15, 15))):
-                moved = pltpu.roll(e[f, p, inner].astype(F32), turn, 0)
+                moved = pltpu.roll(e[f][p, inner].astype(F32), turn, 0)
                 beyond = jnp.broadcast_to(le[side, pl.ds(15 + p, 1), :], (16, EX))
-                e[f, p, outer] = jnp.where(sub == edge, beyond, moved).astype(BF16)
+                e[f][p, outer] = jnp.where(sub == edge, beyond, moved).astype(BF16)
             return 0
 
         lax.fori_loop(0, RO + 2, fill, 0)
-        return 0
 
 
     def partner(i, g, k):
@@ -187,23 +181,25 @@
 
     pl.semaphore_wait(entry, WA - 1)
 
-    def conv(f, _):
+    def conv(f):
         flag = keep[f, 0].astype(F32)
 
         def group(gg, _):
             g = lax.rem(own_g + gg, 4)
+            if f == 0:
+                expand(1, gg * 4, 4)
             for rr in range(0, 4, 2):
                 for n in range(0, EX, 128):
                     taps = [kb[i, :, n : n + 128].astype(BF16)[None] for i in range(10)]
                     for q in range(rr, rr + 2):
                         sums = []
                         for i in range(3):
-                            part = [taps[3 * i + j] * e[f, g * 4 + q + i, j : j + 4, :, n : n + 128] for j in range(3)]
+                            part = [taps[3 * i + j] * e[f][g * 4 + q + i, j : j + 4, :, n : n + 128] for j in range(3)]
                             sums.append(part[0] + part[1] + part[2])
                         acc = (sums[0] + sums[1]) + (sums[2] + taps[9])
                         mx[q * 64 : q * 64 + 64, n : n + 128] = gelu_of_half(acc).reshape(64, 128)
             tokens = xp[f, pl.ds(g * 4, 4)].reshape(256, C)
-            put(fs, slice(None), tokens.astype(F32) + flag * dot(mx[...], wp[...]))
+            put(fs, slice(None), tokens.astype(F32) + flag * dot(mx[0:256], wp[...]))
             for i in range(4):
                 for k in range(8):
                     part = take(fs, pl.ds(i * 64 + k, 8, stride=8))
@@ -213,19 +209,12 @@
 
         lax.fori_loop(0, 4, group, 0)
         r[f, me] = s[f, me]
-        return 0
-
-    def front(f, _):
-        @pl.when(f > 0)
-        def _():
-            expand(f, 0)
-
+
+    for f in range(FR):
         for c in halo(f):
             c.wait()
-        edges(f, 0)
-        return conv(f, 0)
-
-    lax.fori_loop(0, FR, front, 0)
+        edges(f)
+        conv(f)
 
     lane = lax.broadcasted_iota(jnp.int32, (256, 128), 1)
     heads = [(lane >= h * HD) & (lane < (h + 1) * HD) for h in range(4)]
@@ -244,30 +233,30 @@
         put(t, slice(None), r[f].astype(F32).reshape(DEV * 8, C))
         flag = keep[f, 1].astype(F32)
 
-        def window(j, _):
-            first = jnp.concatenate([take(t, pl.ds(2 * j + h, DEV, stride=8)) for h in range(2)], 0)
-            qkv = dot(norm(first), wqkv[...]).astype(BF16)
-            parts = []
-            for grp in range(3):
-                q, k, v = (qkv[:, C * a + 128 * grp : C * a + 128 * grp + 128] for a in range(3))
-                v = jnp.concatenate([v, ones], 1)
-                att = None
-                for h in range(4):
-                    sc = lax.dot_general(q * masks[h], k, (((1,), (1,)), ((), ())), preferred_element_type=F32)
-                    sc = sc - jnp.max(sc, axis=-1, keepdims=True)
-                    pv = dot(jnp.exp2(sc * expo).astype(BF16), v)
-                    pv = pv[:, :128] / pv[:, 128:]
-                    att = pv if att is None else jnp.where(heads[h], pv, att)
-                parts.append(att.astype(BF16))
-            second = first + flag * dot(jnp.concatenate(parts, 1), wo[...])
+        def windows(p, _):
+            rows = [pl.ds(2 * p * UNROLL + i, DEV, stride=8) for i in range(2 * UNROLL)]
+            first = jnp.concatenate([take(t, part) for part in rows], 0)
+            all_qkv = dot(norm(first), wqkv[...]).astype(BF16)
+            whole = []
+            for u in range(UNROLL):
+                qkv = all_qkv[256 * u : 256 * u + 256]
+                parts = []
+                for grp in range(3):
+                    q, k, v = (qkv[:, C * a + 128 * grp : C * a + 128 * grp + 128] for a in range(3))
+                    v = jnp.concatenate([v, ones], 1)
+                    att = None
+                    for h in range(4):
+                        sc = lax.dot_general(q * masks[h], k, (((1,), (1,)), ((), ())), preferred_element_type=F32)
+                        sc = sc - jnp.max(sc, axis=-1, keepdims=True)
+                        pv = dot(jnp.exp2(sc * expo).astype(BF16), v)
+                        pv = pv[:, :128] / pv[:, 128:]
+                        att = pv if att is None else jnp.where(heads[h], pv, att)
+                    parts.append(att.astype(BF16))
+                whole.append(jnp.concatenate(parts, 1))
+            second = first + flag * dot(jnp.concatenate(whole, 0), wo[...])
             second = second.astype(BF16).astype(F32)
-            for h in range(2):
-                put(t, pl.ds(2 * j + h, DEV, stride=8), second[h * DEV : (h + 1) * DEV])
-            return 0
-
-        def windows(p, _):
-            for u in range(UNROLL):
-                window(p * UNROLL + u, 0)
+            for i, part in enumerate(rows):
+                put(t, part, second[i * DEV : (i + 1) * DEV])
             return 0
 
         lax.fori_loop(0, 4 // UNROLL, windows, 0)
@@ -285,16 +274,17 @@
 
         @pl.when(f == 1)
         def _():
-            def block(gg, _):
-                g = lax.rem(own_g + gg, 4)
-                second = jnp.concatenate([take(t, pl.ds((i * 4 + g) * 64, 64)) for i in range(4)], 0)
+            def block(p, _):
+                parts = [i * 4 + lax.rem(own_g + 2 * p + u, 4) for u in range(2) for i in range(4)]
+                second = jnp.concatenate([take(t, pl.ds(part * 64, 64)) for part in parts], 0)
                 res = mlp(second, keep[1, 2].astype(F32))
-                for i in range(4):
-                    z[1, pl.ds((i * 4 + g) * WA, WA)] = res[i * 64 : (i + 1) * 64].reshape(8, 8, C)
-                spread(z.at[1], out.at[1], z_send.at[1], z_recv.at[1], gg)
+                for i, part in enumerate(parts):
+                    z[1, pl.ds(part * WA, WA)] = res[i * 64 : (i + 1) * 64].reshape(8, 8, C)
+                for u in range(2):
+                    spread(z.at[1], out.at[1], z_send.at[1], z_recv.at[1], 2 * p + u)
                 return 0
 
-            lax.fori_loop(0, 4, block, 0)
+            lax.fori_loop(0, 2, block, 0)
             pltpu.make_async_copy(z.at[1, me], out.at[1, me], own.at[1]).start()
 
         return 0
@@ -303,13 +293,13 @@
     arrived(z.at[0], o, z_send.at[0], z_recv.at[0]).wait_recv()
 
     def home(b, _):
-        part = pl.ds(b * 32, 32)
-        second = o[part].astype(F32).reshape(256, C)
-        r[0, part] = mlp(second, keep[0, 2].astype(F32)).reshape(32, 8, C)
+        part = pl.ds(b * 64, 64)
+        second = o[part].astype(F32).reshape(512, C)
+        r[0, part] = mlp(second, keep[0, 2].astype(F32)).reshape(64, 8, C)
         pltpu.make_async_copy(r.at[0, part], out.at[0, part], own.at[0]).start()
         return 0
 
-    lax.fori_loop(0, 4, home, 0)
+    lax.fori_loop(0, 2, home, 0)
     pltpu.make_async_copy(r.at[0], out.at[0], own.at[0]).wait()
     pltpu.make_async_copy(z.at[1, me], out.at[1, me], own.at[1]).wait()
     arrived(z.at[1], out.at[1], z_send.at[1], z_recv.at[1]).wait_recv()
@@ -319,14 +309,13 @@
         arrived(s.at[f], r.at[f], s_send.at[f], s_recv.at[f]).wait_send()
 
 
-def gather(o, out, fs):
+def gather(o, out):
+    to = lax.broadcasted_iota(jnp.int32, (CO, CO), 0)
+    frm = lax.broadcasted_iota(jnp.int32, (CO, CO), 1)
+    order = (frm == 2 * (to % 32) + to // 32).astype(F32).astype(BF16)
     for g in range(o.shape[2]):
         for i in range(4):
-            n = 4 * g + i
-            put(fs, slice(64 * n, 64 * n + 64), o[0, i, g].astype(F32).reshape(64, C))
-            for half in range(2):
-                part = take(fs, pl.ds(64 * n + half, 32, stride=2))
-                out[0, n, half * 32 : half * 32 + 32] = part.astype(BF16)
+            out[0, 4 * g + i] = dot(order, o[0, i, g].reshape(CO, C)).astype(BF16)
 
 
 def body(frames, keep, we, dwk, bias, wp, wqkv, wo, wi, w2):
@@ -343,15 +332,16 @@
             pltpu.VMEM((FR, RO, CO, C), BF16),
             pltpu.VMEM((2, FR, RO, C), BF16),
             pltpu.VMEM((FR, 224, C), BF16),
-            pltpu.VMEM((FR, RO + 2, 6, 16, EX), BF16),
+            pltpu.VMEM((RO + 2, 6, 16, EX), BF16),
+            pltpu.VMEM((RO + 2, 6, 16, EX), BF16),
             pltpu.VMEM((10, 16, EX), F32),
             pltpu.VMEM((2, 48, EX), F32),
-            pltpu.VMEM((256, EX), BF16),
+            pltpu.VMEM((512, EX), BF16),
             slots, slots, slots,
             pltpu.VMEM((DEV, 8, C), BF16),
             pltpu.VMEM((3, DEV * 8, 128), F32),
             pltpu.VMEM((3, 256, 128), F32),
-            dma((len(arrays),)), dma((FR, 8)), dma((FR, 8)),
+            dma((len(arrays) + 1,)), dma((FR, 8)), dma((FR, 8)),
             dma((FR,)), dma((FR,)), dma((FR,)), dma((FR,)), dma((FR,)),
             pltpu.SemaphoreType.REGULAR,
         ],
@@ -360,14 +350,13 @@
         ),
         name="block",
     )(frames, keep, we, dwk, bias, wp, wqkv, wo, wi, w2)
-    steps = 2
+    steps = 1
     return pl.pallas_call(
         gather,
         out_shape=jax.ShapeDtypeStruct(frames.shape, BF16),
         grid=(FR, steps),
         in_specs=[pl.BlockSpec((1, 4, 4 // steps, 8, 8, C), lambda f, g: (f, 0, g, 0, 0, 0))],
         out_specs=pl.BlockSpec((1, RO // steps, CO, C), lambda f, g: (f, g, 0, 0)),
-        scratch_shapes=[pltpu.VMEM((3, RO // steps * CO, 128), F32)],
         name="rows",
     )(result.reshape(FR, 4, 4, 8, 8, C))
 

time: 66.2 us -> 71.3 us (1.077)
  Pallas kernels: 66.1 us -> 71.1 us
    pallas_call x1, Pallas kernels: 62.3 us -> 68.4 us  [body(): pl.pallas_call(kernel, out_shape=jax.ShapeDtypeStruct((FR, DEV, 8, C), BF...]
    pallas_call x1, Pallas kernels: 3.77 us -> 2.75 us  [body(): pl.pallas_call(gather, out_shape=jax.ShapeDtypeStruct(frames.shape, BF16)...]
where the time goes in v4:
time: 71.3 us; the launch traced here: 71.1 us
  Pallas kernels  71.1 us (100%)
    pallas_call x1, Pallas kernels, body(): pl.pallas_call(kernel, out_shape=jax.ShapeDtypeStruct((FR, DEV, 8, C), BF...  68.4 us
    pallas_call x1, Pallas kernels, body(): pl.pallas_call(gather, out_shape=jax.ShapeDtypeStruct(frames.shape, BF16)...  2.75 us

profile of v4, /device:TPU:1, one launch (start us, length us, event | category | flops | bytes accessed | tf_op | source)
XLA Modules:
  0.0 71.1 jit_solution(10659075536847293334)
XLA Ops:
  0.0 68.4 %block.1 = bf16[2,128,8,384]{3,2,1,0:T(8,128)(2,1)} custom-call(bf16[2,16,64,384]{3,2,1,0:T(8,128)(2,1)} %x_hbm.1, s32[2,3]{1,0:T(2,128)} %keep.1, bf16[384,1536]{1,0:T(8,128)(2,1)} %we_hbm.1, f32[3,3,1536]{2,1,0:T(4,128)} %dwk_hbm.1, f32[1536]{0:T(1024)} %bias_hbm.1, bf16[1536,384]{1,0:T(8,128)(2,1)} %wp_hbm.1, bf16[384,1152]{1,0:T(8,128)(2,1)} %wqkv_hbm.1, ...), custom_call_target="tpu_custom_call" | custom-call | tf_op jit(solution)/shard_map/block/pallas_call | solution.py:326
  68.4 2.7 %rows.1 = bf16[2,16,64,384]{3,2,1,0:T(8,128)(2,1)} custom-call(bf16[2,4,4,8,8,384]{5,4,3,2,1,0:T(8,128)(2,1)} %bitcast.1), custom_call_target="tpu_custom_call" | custom-call | tf_op jit(solution)/shard_map/rows/pallas_call | solution.py:354

commit v5 on v4

--- a/solution.py
+++ b/solution.py
@@ -186,8 +186,6 @@
 
         def group(gg, _):
             g = lax.rem(own_g + gg, 4)
-            if f == 0:
-                expand(1, gg * 4, 4)
             for rr in range(0, 4, 2):
                 for n in range(0, EX, 128):
                     taps = [kb[i, :, n : n + 128].astype(BF16)[None] for i in range(10)]
@@ -213,6 +211,9 @@
     for f in range(FR):
         for c in halo(f):
             c.wait()
+        if f == 1:
+            for q in range(2):
+                expand(1, q * 8, 8)
         edges(f)
         conv(f)
 
@@ -224,9 +225,10 @@
 
     def mlp(second, flag):
         normed = norm(second)
+        m = second.shape[0]
         for n in range(0, EX, CH):
-            mx[:, n : n + CH] = gelu(dot(normed, wi[:, n : n + CH]).astype(BF16))
-        return (second + flag * dot(mx[...], w2[...])).astype(BF16)
+            mx[0:m, n : n + CH] = gelu(dot(normed, wi[:, n : n + CH]).astype(BF16))
+        return (second + flag * dot(mx[0:m], w2[...])).astype(BF16)
 
     def attention(f, _):
         arrived(s.at[f], r.at[f], s_send.at[f], s_recv.at[f]).wait_recv()
@@ -275,16 +277,15 @@
         @pl.when(f == 1)
         def _():
             def block(p, _):
-                parts = [i * 4 + lax.rem(own_g + 2 * p + u, 4) for u in range(2) for i in range(4)]
+                parts = [i * 4 + lax.rem(own_g + p, 4) for i in range(4)]
                 second = jnp.concatenate([take(t, pl.ds(part * 64, 64)) for part in parts], 0)
                 res = mlp(second, keep[1, 2].astype(F32))
                 for i, part in enumerate(parts):
                     z[1, pl.ds(part * WA, WA)] = res[i * 64 : (i + 1) * 64].reshape(8, 8, C)
-                for u in range(2):
-                    spread(z.at[1], out.at[1], z_send.at[1], z_recv.at[1], 2 * p + u)
+                spread(z.at[1], out.at[1], z_send.at[1], z_recv.at[1], p)
                 return 0
 
-            lax.fori_loop(0, 2, block, 0)
+            lax.fori_loop(0, 4, block, 0)
             pltpu.make_async_copy(z.at[1, me], out.at[1, me], own.at[1]).start()
 
         return 0

time: 71.3 us -> 63.9 us (0.90)
  Pallas kernels: 71.1 us -> 63.7 us
    pallas_call x1, Pallas kernels: 68.4 us -> 61 us  [body(): pl.pallas_call(kernel, out_shape=jax.ShapeDtypeStruct((FR, DEV, 8, C), BF...]
where the time goes in v5:
time: 63.9 us; the launch traced here: 63.7 us
  Pallas kernels  63.7 us (100%)
    pallas_call x1, Pallas kernels, body(): pl.pallas_call(kernel, out_shape=jax.ShapeDtypeStruct((FR, DEV, 8, C), BF...  61 us
    pallas_call x1, Pallas kernels, body(): pl.pallas_call(gather, out_shape=jax.ShapeDtypeStruct(frames.shape, BF16)...  2.75 us

profile of v5, /device:TPU:1, one launch (start us, length us, event | category | flops | bytes accessed | tf_op | source)
XLA Modules:
  0.0 63.7 jit_solution(13037744745012801688)
XLA Ops:
  0.0 61.0 %block.1 = bf16[2,128,8,384]{3,2,1,0:T(8,128)(2,1)} custom-call(bf16[2,16,64,384]{3,2,1,0:T(8,128)(2,1)} %x_hbm.1, s32[2,3]{1,0:T(2,128)} %keep.1, bf16[384,1536]{1,0:T(8,128)(2,1)} %we_hbm.1, f32[3,3,1536]{2,1,0:T(4,128)} %dwk_hbm.1, f32[1536]{0:T(1024)} %bias_hbm.1, bf16[1536,384]{1,0:T(8,128)(2,1)} %wp_hbm.1, bf16[384,1152]{1,0:T(8,128)(2,1)} %wqkv_hbm.1, ...), custom_call_target="tpu_custom_call" | custom-call | tf_op jit(solution)/shard_map/block/pallas_call | solution.py:327
  61.0 2.7 %rows.1 = bf16[2,16,64,384]{3,2,1,0:T(8,128)(2,1)} custom-call(bf16[2,4,4,8,8,384]{5,4,3,2,1,0:T(8,128)(2,1)} %bitcast.1), custom_call_target="tpu_custom_call" | custom-call | tf_op jit(solution)/shard_map/rows/pallas_call | solution.py:355

commit v6 on v5

--- a/solution.py
+++ b/solution.py
@@ -208,12 +208,12 @@
         lax.fori_loop(0, 4, group, 0)
         r[f, me] = s[f, me]
 
+    expand(1, 0, 8)
     for f in range(FR):
         for c in halo(f):
             c.wait()
         if f == 1:
-            for q in range(2):
-                expand(1, q * 8, 8)
+            expand(1, 8, 8)
         edges(f)
         conv(f)
 

time: 63.9 us -> 67.8 us (1.061)
  Pallas kernels: 63.7 us -> 67.7 us
    pallas_call x1, Pallas kernels: 61 us -> 64.9 us  [body(): pl.pallas_call(kernel, out_shape=jax.ShapeDtypeStruct((FR, DEV, 8, C), BF...]
where the time goes in v6:
time: 67.8 us; the launch traced here: 67.7 us
  Pallas kernels  67.7 us (100%)
    pallas_call x1, Pallas kernels, body(): pl.pallas_call(kernel, out_shape=jax.ShapeDtypeStruct((FR, DEV, 8, C), BF...  64.9 us
    pallas_call x1, Pallas kernels, body(): pl.pallas_call(gather, out_shape=jax.ShapeDtypeStruct(frames.shape, BF16)...  2.75 us

profile of v6, /device:TPU:1, one launch (start us, length us, event | category | flops | bytes accessed | tf_op | source)
XLA Modules:
  0.0 67.7 jit_solution(10472352268944111555)
XLA Ops:
  0.0 64.9 %block.1 = bf16[2,128,8,384]{3,2,1,0:T(8,128)(2,1)} custom-call(bf16[2,16,64,384]{3,2,1,0:T(8,128)(2,1)} %x_hbm.1, s32[2,3]{1,0:T(2,128)} %keep.1, bf16[384,1536]{1,0:T(8,128)(2,1)} %we_hbm.1, f32[3,3,1536]{2,1,0:T(4,128)} %dwk_hbm.1, f32[1536]{0:T(1024)} %bias_hbm.1, bf16[1536,384]{1,0:T(8,128)(2,1)} %wp_hbm.1, bf16[384,1152]{1,0:T(8,128)(2,1)} %wqkv_hbm.1, ...), custom_call_target="tpu_custom_call" | custom-call | tf_op jit(solution)/shard_map/block/pallas_call | solution.py:327
  64.9 2.7 %rows.1 = bf16[2,16,64,384]{3,2,1,0:T(8,128)(2,1)} custom-call(bf16[2,4,4,8,8,384]{5,4,3,2,1,0:T(8,128)(2,1)} %bitcast.1), custom_call_target="tpu_custom_call" | custom-call | tf_op jit(solution)/shard_map/rows/pallas_call | solution.py:355
